TPU v7x, 512 devices: a whole 4x8x8 slice. The times are simulated.
512 devices in a mesh: lang: 64 (over y, z), rep: 8 (over x, core).
Axes of the slice: x: 4, y: 8, z: 8, core: 2. Of those that a mesh axis runs over, the one named last changes fastest.
Arguments:
- tokens: bfloat16 [65536, 1024], P(('lang', 'rep')), may hold values from -24 to 24
- grad_out: bfloat16 [65536, 1024], P(('lang', 'rep')), may hold values from -24 to 24
- lang_ids: int32 [65536], P(('lang', 'rep')), may hold values from 0 to 7, as said below
- slot_ids: int32 [65536], P(('lang', 'rep')), may hold values from 0 to 23, as said below
- w_up: bfloat16 [1024, 32768], P(None, 'lang'), may hold values from -0.1875 to 0.1875
- w_down_t: bfloat16 [1024, 32768], P(None, 'lang'), may hold values from -0.09375 to 0.09375
Outputs:
- ffn_out: bfloat16 [65536, 1024], P(('lang', 'rep'))
- grad_tokens: bfloat16 [65536, 1024], P(('lang', 'rep'))
- grad_up: float32 [1024, 32768], P('rep', 'lang')
- grad_down: float32 [1024, 32768], P('rep', 'lang')
Inputs may be any that keep to these rules, and one draw needn't show every extreme that they name: `lang_ids`: each device holds 128 consecutive tokens. On every device one language, the same on all devices, has exactly 24 tokens; every other language has at most 18 tokens on a device, and on every device one of them has exactly 18. `slot_ids`: on each device the tokens of one language hold the distinct slots 0 to their count minus 1, in no particular order.
All inputs are finite; a program needn't handle non-finite values.
Results may differ from a plain program's by a relative error of at most 0.0058.
Values may be sent and summed in bfloat16 or wider, within the bound.
A program may use at most 128 MiB of HBM per device.

v0:
```python
import functools

import jax
import jax.numpy as jnp
from jax import lax
from jax.experimental import pallas as pl
from jax.experimental.pallas import tpu as pltpu
from jax.sharding import Mesh
from jax.sharding import PartitionSpec as P

MODULES = 8
TOK_DEV = 128
CAPACITY = 18


INV_ROOT_TWO = 0.7071067811865476
INV_ROOT_TAU = 0.3989422804014327


def gelu_value(values):
    return 0.5 * values * (1.0 + lax.erf(values * INV_ROOT_TWO))


def gelu_slope(values):
    return (
        0.5 * (1.0 + lax.erf(values * INV_ROOT_TWO))
        + values * jnp.exp(-0.5 * values * values) * INV_ROOT_TAU
    )

MESH_IDS = pl.DeviceIdType.MESH
VMEM_LIMIT = 48 * 1024 * 1024
PARTS = 3


def enter(n):
    me = lax.axis_index("lz")
    right, left = lax.rem(me + 1, n), lax.rem(me + n - 1, n)
    barrier = pltpu.get_barrier_semaphore()
    for neighbour in (left, right):
        pl.semaphore_signal(barrier, inc=1, device_id={"lz": neighbour}, device_id_type=MESH_IDS)
    pl.semaphore_wait(barrier, 2)
    return me, right, left


def ring_gather_kernel(n, x_ref, o_ref, send_sem, recv_sem):
    me, right, left = enter(n)
    half = x_ref.shape[1] // PARTS
    o_ref[0, me] = x_ref[0]
    o_ref[1, me] = x_ref[1]

    def hop(stream, part, step):
        rows = pl.ds(part * half, half)
        if stream == 0:
            slot, peer = lax.rem(me - step + n, n), right
        else:
            slot, peer = lax.rem(me + step, n), left
        src = x_ref.at[stream, rows] if step == 0 else o_ref.at[stream, slot, rows]
        return pltpu.make_async_remote_copy(
            src_ref=src, dst_ref=o_ref.at[stream, slot, rows],
            send_sem=send_sem.at[stream, part, step], recv_sem=recv_sem.at[stream, part, step],
            device_id={"lz": peer}, device_id_type=MESH_IDS)

    order = [(stream, part) for part in range(PARTS) for stream in range(2)]
    copies = []
    last = {}
    for key in order:
        last[key] = hop(*key, 0)
        last[key].start()
        copies.append(last[key])
    for step in range(1, n - 1):
        for key in order:
            last[key].wait_recv()
            last[key] = hop(*key, step)
            last[key].start()
            copies.append(last[key])
    for key in order:
        last[key].wait_recv()
    for copy in copies:
        copy.wait_send()


def ring_gather(x, n):
    two, rows, width = x.shape
    return pl.pallas_call(
        functools.partial(ring_gather_kernel, n),
        out_shape=jax.ShapeDtypeStruct((two, n, rows, width), x.dtype),
        in_specs=[pl.BlockSpec(memory_space=pltpu.VMEM)],
        out_specs=pl.BlockSpec(memory_space=pltpu.VMEM),
        scratch_shapes=[pltpu.SemaphoreType.DMA((2, PARTS, n - 1)), pltpu.SemaphoreType.DMA((2, PARTS, n - 1))],
        compiler_params=pltpu.CompilerParams(
            collective_id=0, has_side_effects=True, vmem_limit_bytes=VMEM_LIMIT),
    )(x)


def ring_sum_kernel(n, pa_ref, pb_ref, o_ref, first_r, first_l, send_r, send_l, recv_r, recv_l,
                    send_sem, recv_sem):
    me, right, left = enter(n)
    half = pa_ref.shape[1] // PARTS
    parts = (pa_ref, pb_ref)
    sends = (send_r, send_l)
    recvs = (recv_r, recv_l)

    def chunk_for(stream, step):
        if stream == 0:
            return lax.rem(me + 2 * n - 1 - step, n)
        return lax.rem(me + 1 + step, n)

    firsts = (first_r, first_l)

    def hop(stream, part, step):
        rows = pl.ds(part * half, half)
        if step == 0:
            src = parts[stream].at[chunk_for(stream, 0), rows]
            dst = firsts[stream].at[rows]
        else:
            src, dst = sends[stream].at[step, rows], recvs[stream].at[step, rows]
        return pltpu.make_async_remote_copy(
            src_ref=src, dst_ref=dst,
            send_sem=send_sem.at[stream, part, step], recv_sem=recv_sem.at[stream, part, step],
            device_id={"lz": right if stream == 0 else left}, device_id_type=MESH_IDS)

    order = [(stream, part) for part in range(PARTS) for stream in range(2)]
    copies = []
    last = {}
    for stream, part in order:
        last[stream, part] = hop(stream, part, 0)
        last[stream, part].start()
        copies.append(last[stream, part])
    for step in range(1, n - 1):
        for stream, part in order:
            rows = pl.ds(part * half, half)
            last[stream, part].wait_recv()
            if step == 1:
                came = firsts[stream][rows].astype(jnp.float32)
            else:
                came = recvs[stream][step - 1, rows]
            sends[stream][step, rows] = came + parts[stream][chunk_for(stream, step), rows].astype(
                jnp.float32)
            last[stream, part] = hop(stream, part, step)
            last[stream, part].start()
            copies.append(last[stream, part])
    for stream, part in order:
        rows = pl.ds(part * half, half)
        last[stream, part].wait_recv()
        o_ref[stream, rows] = (
            recvs[stream][n - 2, rows] + parts[stream][me, rows].astype(jnp.float32)
        ).astype(o_ref.dtype)
    for copy in copies:
        copy.wait_send()


def ring_sum(first, second, n):
    _, rows, width = first.shape
    return pl.pallas_call(
        functools.partial(ring_sum_kernel, n),
        out_shape=jax.ShapeDtypeStruct((2, rows, width), first.dtype),
        in_specs=[pl.BlockSpec(memory_space=pltpu.VMEM)] * 2,
        out_specs=pl.BlockSpec(memory_space=pltpu.VMEM),
        scratch_shapes=[pltpu.VMEM((rows, width), first.dtype)] * 2
        + [pltpu.VMEM((n - 1, rows, width), jnp.float32)] * 4
        + [pltpu.SemaphoreType.DMA((2, PARTS, n - 1)), pltpu.SemaphoreType.DMA((2, PARTS, n - 1))],
        compiler_params=pltpu.CompilerParams(
            collective_id=1, has_side_effects=True, vmem_limit_bytes=VMEM_LIMIT),
    )(first, second)


def y_exchange_kernel(n_y, x_ref, o_ref, send_sem, recv_sem):
    me = lax.axis_index("ly")
    barrier = pltpu.get_barrier_semaphore()
    for k in range(1, n_y):
        pl.semaphore_signal(
            barrier, inc=1, device_id={"ly": lax.rem(me + k, n_y)}, device_id_type=MESH_IDS)
    pl.semaphore_wait(barrier, n_y - 1)

    def exchange(k, src, dst):
        return pltpu.make_async_remote_copy(
            src_ref=src, dst_ref=dst, send_sem=send_sem.at[k], recv_sem=recv_sem.at[k],
            device_id={"ly": lax.rem(me + k, n_y)}, device_id_type=MESH_IDS)

    copies = []
    for k in range(1, n_y):
        copy = exchange(k, x_ref.at[:, lax.rem(me + k, n_y)], o_ref.at[:, me])
        copy.start()
        copies.append(copy)
    o_ref[:, me] = x_ref[:, me]
    for k in range(1, n_y):
        exchange(k, x_ref.at[:, me], o_ref.at[:, lax.rem(me + n_y - k, n_y)]).wait_recv()
    for copy in copies:
        copy.wait_send()


def y_exchange(x, call_id):
    n_y = x.shape[1]
    return pl.pallas_call(
        functools.partial(y_exchange_kernel, n_y),
        out_shape=jax.ShapeDtypeStruct(x.shape, x.dtype),
        in_specs=[pl.BlockSpec(memory_space=pltpu.VMEM)],
        out_specs=pl.BlockSpec(memory_space=pltpu.VMEM),
        scratch_shapes=[pltpu.SemaphoreType.DMA((n_y,)), pltpu.SemaphoreType.DMA((n_y,))],
        compiler_params=pltpu.CompilerParams(
            collective_id=call_id, has_side_effects=True, vmem_limit_bytes=VMEM_LIMIT),
    )(x)


def per_device(tokens, grad_out, lang_ids, slot_ids, w_up, w_down_t):
    feature_width = tokens.shape[1]
    capacity = CAPACITY
    keep_mask = slot_ids < capacity
    target = jnp.where(keep_mask, lang_ids * capacity + slot_ids, MODULES * capacity)
    safe_slot = jnp.minimum(slot_ids, capacity - 1)
    token_scale = 1.0 / TOK_DEV

    def place(values):
        buffer = (
            jnp.zeros((MODULES * capacity, feature_width), values.dtype)
            .at[target]
            .set(values, mode="drop")
        )
        return buffer.reshape(MODULES, capacity, feature_width)

    n_z = lax.axis_size("lz")

    def dispatch(first, second):
        both = jnp.stack([place(first), place(second)])
        lanes = 128
        by_y = y_exchange(both.reshape(2, MODULES, -1, lanes), 2)
        every = ring_gather(by_y.reshape(2, -1, feature_width), n_z)
        every = every.reshape(2, -1, feature_width)
        return every[0], every[1]

    def give_back(first, second):
        summed = ring_sum(
            first.reshape(n_z, -1, feature_width), second.reshape(n_z, -1, feature_width), n_z)
        summed = summed.reshape(2, -1, capacity, feature_width)
        back = y_exchange(summed.reshape(2, MODULES, -1, 128), 3)
        back = back.reshape(2, MODULES, capacity, feature_width)
        return back[0], back[1]

    def collect(returned):
        picked = returned[lang_ids, safe_slot]
        return jnp.where(keep_mask[:, None], picked, jnp.zeros_like(picked))

    flat_tokens, flat_grads = dispatch(tokens, grad_out)
    pre_flat = jnp.dot(flat_tokens, w_up, preferred_element_type=jnp.float32)
    hidden_flat = gelu_value(pre_flat).astype(jnp.bfloat16)
    partial_rows = lax.dot_general(
        hidden_flat, w_down_t, (((1,), (1,)), ((), ())), preferred_element_type=jnp.float32
    ).astype(jnp.bfloat16)
    grad_down = lax.psum_scatter(
        lax.dot_general(
            flat_grads, hidden_flat, (((0,), (0,)), ((), ())), preferred_element_type=jnp.float32
        )
        * token_scale,
        "rep",
        scatter_dimension=0,
        tiled=True,
    )
    d_hidden = jnp.dot(flat_grads, w_down_t, preferred_element_type=jnp.float32)
    d_pre = (d_hidden * gelu_slope(pre_flat)).astype(jnp.bfloat16)
    grad_up = lax.psum_scatter(
        lax.dot_general(
            flat_tokens, d_pre, (((0,), (0,)), ((), ())), preferred_element_type=jnp.float32
        )
        * token_scale,
        "rep",
        scatter_dimension=0,
        tiled=True,
    )
    dx_part = lax.dot_general(
        d_pre, w_up, (((1,), (1,)), ((), ())), preferred_element_type=jnp.float32
    ).astype(jnp.bfloat16)
    returned, dx_back = give_back(partial_rows, dx_part)
    return (collect(returned), collect(dx_back), grad_up, grad_down)


def solution(mesh):
    n_lang = mesh.shape["lang"]
    groups = n_lang // MODULES
    devices = mesh.devices.reshape(MODULES, groups, mesh.shape["rep"])
    split_mesh = Mesh(devices, ("ly", "lz", "rep"))
    rows = P(("ly", "lz", "rep"), None)
    ids = P(("ly", "lz", "rep"))
    cols = P(None, ("ly", "lz"))
    return jax.shard_map(
        per_device,
        mesh=split_mesh,
        in_specs=(rows, rows, ids, ids, cols, cols),
        out_specs=(rows, rows, P("rep", ("ly", "lz")), P("rep", ("ly", "lz"))),
        check_vma=False,
    )
```

profile of v0, /device:TPU:6, one launch (start us, length us, event | category | flops | bytes accessed | tf_op | source)
XLA Modules:
  0.0 221.2 jit_solution(8341503183228198442)
XLA Ops:
  7.2 0.0 copy-start
  7.2 0.0 reduce-scatter.3.cloned.1.call-start
  7.2 0.8 fusion.11
  8.0 1.6 scatter_custom_fusion
  9.6 0.1 stack.7
  9.8 1.6 scatter_custom_fusion.1
  11.4 0.1 stack.8
  11.5 0.1 pad_maximum_fusion.x_ref
  11.6 20.5 %shard_map.93 = bf16[2,8,144,128]{3,2,1,0:T(8,128)(2,1)S(1)} custom-call(bf16[2,8,144,128]{3,2,1,0:T(8,128)(2,1)S(1)} %pad_maximum_fusion.x_ref), custom_call_target="tpu_custom_call" | custom-call | tf_op jit(solution)/shard_map/pallas_call | solution.py:194
  32.1 0.3 reshape.33.x_ref
  32.4 55.3 %shard_map.94 = bf16[2,8,144,1024]{3,2,1,0:T(8,128)(2,1)S(1)} custom-call(bf16[2,144,1024]{2,1,0:T(8,128)(2,1)S(1)} %reshape.33.x_ref), custom_call_target="tpu_custom_call" | custom-call | tf_op jit(solution)/shard_map/pallas_call | solution.py:84
  87.7 0.7 fusion.14
  88.4 0.0 copy-done
  88.4 0.0 copy-start.2
  88.4 2.6 %multiply_convert_fusion = (bf16[1152,512]{1,0:T(8,128)(2,1)}, f32[1152,512]{1,0:T(8,128)S(1)}) fusion(bf16[1152,1024]{1,0:T(8,128)(2,1)S(1)} %bitcast.28, bf16[1024,512]{1,0:T(8,128)(2,1)S(1)} %copy-done), kind=kOutput, calls=%fused_computation.13 | convolution fusion | flops 1210908672 | bytes 6946816 | tf_op jit(solution)/shard_map/dot_general | solution.py:244
  91.0 0.0 copy-done.2
  91.0 2.0 fusion
  93.1 0.0 copy-start.5
  93.1 1.0 copy-done.5
  94.1 2.9 %convolution_multiply_fusion.2 = f32[1024,512]{1,0:T(8,128)} fusion(bf16[1152,1024]{1,0:T(8,128)(2,1)S(1)} %bitcast.29, bf16[1152,512]{1,0:T(8,128)(2,1)S(1)} %fusion), kind=kOutput, calls=%fused_computation.16 | convolution fusion | flops 1208483840 | bytes 5636096 | tf_op jit(solution)/shard_map/dot_general | solution.py:261
  97.0 0.0 reduce-scatter.3.cloned.1.call-update
  97.0 0.2 reduce-scatter.5.cloned.1.call-start
  97.3 4.1 %convolution_multiply_fusion.1 = f32[1024,512]{1,0:T(8,128)} fusion(bf16[1152,1024]{1,0:T(8,128)(2,1)S(1)} %bitcast.27, bf16[1152,512]{1,0:T(8,128)(2,1)} %get-tuple-element.12), kind=kOutput, calls=%fused_computation.15 | convolution fusion | flops 1208483840 | bytes 5636096 | tf_op jit(solution)/shard_map/dot_general | solution.py:250
  101.4 0.0 reduce-scatter.5.cloned.1.call-update
  101.5 0.0 copy-start.3
  101.5 0.0 copy-start.4
  101.5 2.8 %convolution_convert_fusion = bf16[1152,1024]{1,0:T(8,128)(2,1)S(1)} fusion(bf16[1152,512]{1,0:T(8,128)(2,1)} %copy-done.5, bf16[1024,512]{1,0:T(8,128)(2,1)S(1)} %copy-done), kind=kOutput, calls=%fused_computation.4 | convolution fusion | flops 1209139200 | bytes 4587520 | tf_op jit(solution)/shard_map/dot_general | solution.py:269
  104.3 0.0 copy-done.3
  104.3 0.0 copy-done.4
  104.3 1.4 convolution_convert_fusion.1
  105.8 86.0 %shard_map.95 = bf16[2,144,1024]{2,1,0:T(8,128)(2,1)S(1)} custom-call(bf16[8,144,1024]{2,1,0:T(8,128)(2,1)S(1)} %bitcast.25, bf16[8,144,1024]{2,1,0:T(8,128)(2,1)S(1)} %bitcast.24), custom_call_target="tpu_custom_call" | custom-call | tf_op jit(solution)/shard_map/pallas_call | solution.py:154
  191.7 0.3 reshape_reshape.3.x_ref
  192.0 17.4 %shard_map.96 = bf16[2,8,144,128]{3,2,1,0:T(8,128)(2,1)S(1)} custom-call(bf16[2,8,144,128]{3,2,1,0:T(8,128)(2,1)S(1)} %reshape_reshape.3.x_ref), custom_call_target="tpu_custom_call" | custom-call | tf_op jit(solution)/shard_map/pallas_call | solution.py:194
  209.5 0.2 squeeze.15
  209.6 0.2 copy.13
  209.8 0.2 squeeze.14
  210.0 0.2 copy.12
  210.2 0.0 copy-start.1
  210.2 1.6 gather_fusion.1
  211.8 1.6 gather_fusion
  213.4 0.0 copy-done.1
  213.4 0.9 broadcast_select_fusion
  214.3 0.0 reduce-scatter.3.cloned.1.call-done
  214.3 0.0 reduce-scatter.5.cloned.1.call-done
  (2 shorter events, 0.0 us)
Async XLA Ops:
  7.2 81.2 %copy-start = (bf16[1024,512]{1,0:T(8,128)(2,1)S(1)}, bf16[1024,512]{1,0:T(8,128)(2,1)}, u32[]{:S(2)}) copy-start(bf16[1024,512]{1,0:T(8,128)(2,1)} %param.10) | copy-start | bytes 3145732
  7.2 207.1 %reduce-scatter.3.cloned.1.call-start = ((), (), s32[]{:S(2)}) async-start(), calls=%async_computation.2 | async-start | bytes 2359296 | tf_op jit(solution)/shard_map/reduce_scatter | solution.py:260
  88.4 2.6 %copy-start.2 = (bf16[1024,512]{1,0:T(8,128)(2,1)S(1)}, bf16[1024,512]{1,0:T(8,128)(2,1)}, u32[]{:S(2)}) copy-start(bf16[1024,512]{1,0:T(8,128)(2,1)} %param.11) | copy-start | bytes 3145732
  93.1 1.0 copy-start.5
  97.0 117.3 %reduce-scatter.5.cloned.1.call-start = ((), (), s32[]{:S(2)}) async-start(), calls=%async_computation.3 | async-start | bytes 2359296 | tf_op jit(solution)/shard_map/reduce_scatter | solution.py:249
  101.5 2.9 %copy-start.3 = (bf16[1024,512]{1,0:T(8,128)(2,1)S(1)}, bf16[1024,512]{1,0:T(8,128)(2,1)}, u32[]{:S(2)}) copy-start(bf16[1024,512]{1,0:T(8,128)(2,1)} %param.11) | copy-start | bytes 3145732
  101.5 2.9 %copy-start.4 = (bf16[1152,512]{1,0:T(8,128)(2,1)S(1)}, bf16[1152,512]{1,0:T(8,128)(2,1)}, u32[]{:S(2)}) copy-start(bf16[1152,512]{1,0:T(8,128)(2,1)} %get-tuple-element.12) | copy-start | bytes 3538948
  210.2 3.2 %copy-start.1 = (s32[128]{0:T(128)S(1)}, s32[128]{0:T(128)}, u32[]{:S(2)}) copy-start(s32[128]{0:T(128)} %param.9) | copy-start | bytes 1540
Sparse Core Ops, SparseCore 0:
  97.2 32.0 reduce-scatter.2
  132.7 38.3 reduce-scatter.4
where the time goes:
time: 222 us; the launch traced here: 221 us
  Pallas kernels  179 us (81%)
  matrix products  16 us (7%)
  between operations  14.3 us (6%)
  local copies, waits for them, and re-layouts  9.71 us (4%)
    pallas_call x1, Pallas kernels, ring_sum(): pl.pallas_call(functools.partial(ring_sum_kernel, n), out_shape=jax.Shape...  86 us
    pallas_call x1, Pallas kernels, ring_gather(): pl.pallas_call(functools.partial(ring_gather_kernel, n), out_shape=jax.Sh...  55.3 us
    pallas_call x2, Pallas kernels, y_exchange(): pl.pallas_call(functools.partial(y_exchange_kernel, n_y), out_shape=jax.S...  37.9 us
  transfers between devices with their start and end apart: 2, of which 0 were waited for; matrix products, arithmetic and copies ran while one was open for 6% of the time, Pallas kernels for 47%

commit v1 on v0

--- a/solution.py
+++ b/solution.py
@@ -28,18 +28,33 @@
     )
 
 MESH_IDS = pl.DeviceIdType.MESH
-VMEM_LIMIT = 48 * 1024 * 1024
+VMEM_LIMIT = 60 * 1024 * 1024
 PARTS = 3
 
 
-def enter(n):
+def enter(n, others=()):
     me = lax.axis_index("lz")
     right, left = lax.rem(me + 1, n), lax.rem(me + n - 1, n)
+    peers = [("lz", left), ("lz", right)] + list(others)
     barrier = pltpu.get_barrier_semaphore()
-    for neighbour in (left, right):
-        pl.semaphore_signal(barrier, inc=1, device_id={"lz": neighbour}, device_id_type=MESH_IDS)
-    pl.semaphore_wait(barrier, 2)
+    for axis, neighbour in peers:
+        pl.semaphore_signal(barrier, inc=1, device_id={axis: neighbour}, device_id_type=MESH_IDS)
+    pl.semaphore_wait(barrier, len(peers))
     return me, right, left
+
+
+def rep_ring(n_r):
+    rep = lax.axis_index("rep")
+    chips = n_r // 2
+    x, core = rep // 2, lax.rem(rep, 2)
+    pos = core * (x + 1) + (1 - core) * lax.rem(n_r - x, n_r)
+
+    def rep_at(p):
+        p = lax.rem(p + 2 * n_r, n_r)
+        up = 1 - lax.rem(p + n_r - 1, n_r) // chips
+        return 2 * (up * (p - 1) + (1 - up) * lax.rem(n_r - p, n_r)) + up
+
+    return pos, rep_at
 
 
 def ring_gather_kernel(n, x_ref, o_ref, send_sem, recv_sem):
@@ -92,9 +107,43 @@
     )(x)
 
 
-def ring_sum_kernel(n, pa_ref, pb_ref, o_ref, first_r, first_l, send_r, send_l, recv_r, recv_l,
-                    send_sem, recv_sem):
-    me, right, left = enter(n)
+def ring_sum_kernel(n, n_r, pa_ref, pb_ref, gd_ref, gu_ref, o_ref, od_ref, ou_ref, first_r, first_l,
+                    send_r, send_l, recv_r, recv_l, send_sem, recv_sem,
+                    gsend_f, gsend_b, grecv_f, grecv_b, gsend_sem, grecv_sem):
+    pos, rep_at = rep_ring(n_r)
+    ahead, behind = rep_at(pos + 1), rep_at(pos - 1)
+    me, right, left = enter(n, [("rep", ahead), ("rep", behind)])
+    block = od_ref.shape[0]
+    grads = (gd_ref, gu_ref)
+    gsends = (gsend_f, gsend_b)
+    grecvs = (grecv_f, grecv_b)
+
+    def grad_rows(stream, step):
+        dest = pos - 1 - step if stream == 0 else pos + 1 + step
+        return pl.ds(pl.multiple_of(rep_at(dest) * block, block), block)
+
+    def grad_hop(stream, step):
+        if step == 0:
+            src = grads[stream].at[grad_rows(stream, 0)]
+        else:
+            src = gsends[stream].at[step]
+        return pltpu.make_async_remote_copy(
+            src_ref=src, dst_ref=grecvs[stream].at[step],
+            send_sem=gsend_sem.at[stream, step], recv_sem=grecv_sem.at[stream, step],
+            device_id={"rep": ahead if stream == 0 else behind}, device_id_type=MESH_IDS)
+
+    grad_copies = []
+    grad_last = {}
+
+    def grad_step(step):
+        for stream in range(2):
+            if step > 0:
+                grad_last[stream].wait_recv()
+                gsends[stream][step] = grecvs[stream][step - 1] + grads[stream][grad_rows(stream, step)]
+            grad_last[stream] = grad_hop(stream, step)
+            grad_last[stream].start()
+            grad_copies.append(grad_last[stream])
+
     half = pa_ref.shape[1] // PARTS
     parts = (pa_ref, pb_ref)
     sends = (send_r, send_l)
@@ -126,7 +175,12 @@
         last[stream, part] = hop(stream, part, 0)
         last[stream, part].start()
         copies.append(last[stream, part])
-    for step in range(1, n - 1):
+    grad_step(0)
+    for step in range(1, max(n, n_r) - 1):
+        if step < n_r - 1:
+            grad_step(step)
+        if step >= n - 1:
+            continue
         for stream, part in order:
             rows = pl.ds(part * half, half)
             last[stream, part].wait_recv()
@@ -145,23 +199,35 @@
         o_ref[stream, rows] = (
             recvs[stream][n - 2, rows] + parts[stream][me, rows].astype(jnp.float32)
         ).astype(o_ref.dtype)
-    for copy in copies:
+    own = pl.ds(pl.multiple_of(rep_at(pos) * block, block), block)
+    for stream, out in ((0, od_ref), (1, ou_ref)):
+        grad_last[stream].wait_recv()
+        out[...] = grecvs[stream][n_r - 2] + grads[stream][own]
+    for copy in copies + grad_copies:
         copy.wait_send()
 
 
-def ring_sum(first, second, n):
+def ring_sum(first, second, grad_d, grad_u, n, n_r):
     _, rows, width = first.shape
+    d_rows, d_cols = grad_d.shape
+    block = d_rows // n_r
     return pl.pallas_call(
-        functools.partial(ring_sum_kernel, n),
-        out_shape=jax.ShapeDtypeStruct((2, rows, width), first.dtype),
-        in_specs=[pl.BlockSpec(memory_space=pltpu.VMEM)] * 2,
-        out_specs=pl.BlockSpec(memory_space=pltpu.VMEM),
+        functools.partial(ring_sum_kernel, n, n_r),
+        out_shape=(
+            jax.ShapeDtypeStruct((2, rows, width), first.dtype),
+            jax.ShapeDtypeStruct((block, d_cols), grad_d.dtype),
+            jax.ShapeDtypeStruct((block, d_cols), grad_u.dtype),
+        ),
+        in_specs=[pl.BlockSpec(memory_space=pltpu.VMEM)] * 4,
+        out_specs=[pl.BlockSpec(memory_space=pltpu.VMEM)] * 3,
         scratch_shapes=[pltpu.VMEM((rows, width), first.dtype)] * 2
         + [pltpu.VMEM((n - 1, rows, width), jnp.float32)] * 4
-        + [pltpu.SemaphoreType.DMA((2, PARTS, n - 1)), pltpu.SemaphoreType.DMA((2, PARTS, n - 1))],
+        + [pltpu.SemaphoreType.DMA((2, PARTS, n - 1)), pltpu.SemaphoreType.DMA((2, PARTS, n - 1))]
+        + [pltpu.VMEM((n_r - 1, block, d_cols), jnp.float32)] * 4
+        + [pltpu.SemaphoreType.DMA((2, n_r - 1)), pltpu.SemaphoreType.DMA((2, n_r - 1))],
         compiler_params=pltpu.CompilerParams(
             collective_id=1, has_side_effects=True, vmem_limit_bytes=VMEM_LIMIT),
-    )(first, second)
+    )(first, second, grad_d, grad_u)
 
 
 def y_exchange_kernel(n_y, x_ref, o_ref, send_sem, recv_sem):
@@ -228,13 +294,14 @@
         every = every.reshape(2, -1, feature_width)
         return every[0], every[1]
 
-    def give_back(first, second):
-        summed = ring_sum(
-            first.reshape(n_z, -1, feature_width), second.reshape(n_z, -1, feature_width), n_z)
+    def give_back(first, second, grad_d, grad_u):
+        summed, grad_d, grad_u = ring_sum(
+            first.reshape(n_z, -1, feature_width), second.reshape(n_z, -1, feature_width),
+            grad_d, grad_u, n_z, lax.axis_size("rep"))
         summed = summed.reshape(2, -1, capacity, feature_width)
         back = y_exchange(summed.reshape(2, MODULES, -1, 128), 3)
         back = back.reshape(2, MODULES, capacity, feature_width)
-        return back[0], back[1]
+        return back[0], back[1], grad_d, grad_u
 
     def collect(returned):
         picked = returned[lang_ids, safe_slot]
@@ -246,30 +313,18 @@
     partial_rows = lax.dot_general(
         hidden_flat, w_down_t, (((1,), (1,)), ((), ())), preferred_element_type=jnp.float32
     ).astype(jnp.bfloat16)
-    grad_down = lax.psum_scatter(
-        lax.dot_general(
-            flat_grads, hidden_flat, (((0,), (0,)), ((), ())), preferred_element_type=jnp.float32
-        )
-        * token_scale,
-        "rep",
-        scatter_dimension=0,
-        tiled=True,
-    )
+    grad_down = lax.dot_general(
+        flat_grads, hidden_flat, (((0,), (0,)), ((), ())), preferred_element_type=jnp.float32
+    ) * token_scale
     d_hidden = jnp.dot(flat_grads, w_down_t, preferred_element_type=jnp.float32)
     d_pre = (d_hidden * gelu_slope(pre_flat)).astype(jnp.bfloat16)
-    grad_up = lax.psum_scatter(
-        lax.dot_general(
-            flat_tokens, d_pre, (((0,), (0,)), ((), ())), preferred_element_type=jnp.float32
-        )
-        * token_scale,
-        "rep",
-        scatter_dimension=0,
-        tiled=True,
-    )
+    grad_up = lax.dot_general(
+        flat_tokens, d_pre, (((0,), (0,)), ((), ())), preferred_element_type=jnp.float32
+    ) * token_scale
     dx_part = lax.dot_general(
         d_pre, w_up, (((1,), (1,)), ((), ())), preferred_element_type=jnp.float32
     ).astype(jnp.bfloat16)
-    returned, dx_back = give_back(partial_rows, dx_part)
+    returned, dx_back, grad_down, grad_up = give_back(partial_rows, dx_part, grad_down, grad_up)
     return (collect(returned), collect(dx_back), grad_up, grad_down)
 
 

time: 222 us -> 229 us (1.032)
  Pallas kernels: 179 us -> 193 us
  between operations: 14.3 us -> 0.84 us
  local copies, waits for them, and re-layouts: 9.71 us -> 17 us
    pallas_call x1, Pallas kernels: 86 us -> 92.8 us  [ring_sum(): pl.pallas_call(functools.partial(ring_sum_kernel, n, n_r), out_shape=(jax...]
    pallas_call x2, Pallas kernels: 37.9 us -> 41.9 us  [y_exchange(): pl.pallas_call(functools.partial(y_exchange_kernel, n_y), out_shape=jax.S...]
    pallas_call x1, Pallas kernels: 55.3 us -> 58.2 us  [ring_gather(): pl.pallas_call(functools.partial(ring_gather_kernel, n), out_shape=jax.Sh...]
  transfers between devices with their start and end apart: 2 -> 0, of which waited for: 0 -> 0; matrix products, arithmetic and copies ran while one was open for 6% -> 0% of each run, Pallas kernels for 47% -> 0%
where the time goes in v1:
time: 229 us; the launch traced here: 228 us
  Pallas kernels  193 us (84%)
  local copies, waits for them, and re-layouts  17 us (7%)
  matrix products  15.2 us (7%)
  other arithmetic  2.54 us (1%)
    pallas_call x1, Pallas kernels, ring_sum(): pl.pallas_call(functools.partial(ring_sum_kernel, n, n_r), out_shape=(jax...  92.8 us
    pallas_call x1, Pallas kernels, ring_gather(): pl.pallas_call(functools.partial(ring_gather_kernel, n), out_shape=jax.Sh...  58.2 us
    pallas_call x2, Pallas kernels, y_exchange(): pl.pallas_call(functools.partial(y_exchange_kernel, n_y), out_shape=jax.S...  41.9 us

profile of v1, /device:TPU:6, one launch (start us, length us, event | category | flops | bytes accessed | tf_op | source)
XLA Modules:
  0.0 228.5 jit_solution(670714460490552863)
XLA Ops:
  0.6 0.0 copy-start
  0.6 0.8 fusion.11
  1.4 1.6 scatter_custom_fusion
  3.1 0.1 stack.7
  3.2 1.6 scatter_custom_fusion.1
  4.8 0.1 stack.8
  5.0 0.9 pad_maximum_fusion.x_ref
  5.8 22.3 %shard_map.93 = bf16[2,8,144,128]{3,2,1,0:T(8,128)(2,1)} custom-call(bf16[2,8,144,128]{3,2,1,0:T(8,128)(2,1)} %pad_maximum_fusion.x_ref), custom_call_target="tpu_custom_call" | custom-call | tf_op jit(solution)/shard_map/pallas_call | solution.py:260
  28.1 2.1 reshape.33.x_ref
  30.3 58.2 %shard_map.94 = bf16[2,8,144,1024]{3,2,1,0:T(8,128)(2,1)} custom-call(bf16[2,144,1024]{2,1,0:T(8,128)(2,1)} %reshape.33.x_ref), custom_call_target="tpu_custom_call" | custom-call | tf_op jit(solution)/shard_map/pallas_call | solution.py:99
  88.4 2.9 %fusion.14 = (bf16[1,8,144,1024]{3,2,1,0:T(8,128)(2,1)S(1)}, bf16[1,8,144,1024]{3,2,1,0:T(8,128)(2,1)S(1)}) fusion(bf16[2,8,144,1024]{3,2,1,0:T(8,128)(2,1)} %shard_map.94), kind=kLoop, calls=%fused_computation.33 | loop fusion | bytes 9437184 | tf_op jit(solution)/shard_map/slice | solution.py:295
  91.3 0.0 copy-done
  91.3 0.0 copy-start.4
  91.4 1.6 multiply_convert_fusion
  92.9 0.0 copy-done.4
  93.0 2.1 fusion
  95.0 3.0 %convolution_multiply_fusion.1.gu_ref = f32[1024,512]{1,0:T(8,128)} fusion(bf16[1152,1024]{1,0:T(8,128)(2,1)S(1)} %bitcast.25, bf16[1152,512]{1,0:T(8,128)(2,1)S(1)} %fusion), kind=kOutput, calls=%fused_computation.15 | convolution fusion | flops 1208483840 | bytes 5636096 | tf_op jit(solution)/shard_map/dot_general | solution.py:321
  98.0 2.9 %convolution_multiply_fusion.2.gd_ref = f32[1024,512]{1,0:T(8,128)} fusion(bf16[1152,1024]{1,0:T(8,128)(2,1)S(1)} %bitcast.23, bf16[1152,512]{1,0:T(8,128)(2,1)S(1)} %get-tuple-element.18), kind=kOutput, calls=%fused_computation.16 | convolution fusion | flops 1208483840 | bytes 5636096 | tf_op jit(solution)/shard_map/dot_general | solution.py:316
  100.9 2.8 %convolution_convert_fusion = bf16[1152,1024]{1,0:T(8,128)(2,1)} fusion(bf16[1152,512]{1,0:T(8,128)(2,1)S(1)} %fusion, bf16[1024,512]{1,0:T(8,128)(2,1)S(1)} %copy-done), kind=kOutput, calls=%fused_computation.4 | convolution fusion | flops 1209139200 | bytes 4587520 | tf_op jit(solution)/shard_map/dot_general | solution.py:324
  103.8 2.8 %convolution_convert_fusion.1 = bf16[1152,1024]{1,0:T(8,128)(2,1)} fusion(bf16[1152,512]{1,0:T(8,128)(2,1)S(1)} %get-tuple-element.18, bf16[1024,512]{1,0:T(8,128)(2,1)S(1)} %copy-done.4), kind=kOutput, calls=%fused_computation.5 | convolution fusion | flops 1209139200 | bytes 4587520 | tf_op jit(solution)/shard_map/dot_general | solution.py:313
  106.6 92.8 %shard_map.95 = (bf16[2,144,1024]{2,1,0:T(8,128)(2,1)}, f32[128,512]{1,0:T(8,128)}, f32[128,512]{1,0:T(8,128)}) custom-call(bf16[8,144,1024]{2,1,0:T(8,128)(2,1)} %bitcast.27, bf16[8,144,1024]{2,1,0:T(8,128)(2,1)} %bitcast.26, f32[1024,512]{1,0:T(8,128)} %convolution_multiply_fusion.2.gd_ref, f32[1024,512]{1,0:T(8,128)} %convolution_multiply_fusion.1.gu_ref), custom_call_target="tpu_custom_call" | custom-call | tf_op jit(solution)/shard_map/pallas_call | solution.py:214
  199.4 2.1 reshape_reshape.3.x_ref
  201.5 19.6 %shard_map.96 = bf16[2,8,144,128]{3,2,1,0:T(8,128)(2,1)} custom-call(bf16[2,8,144,128]{3,2,1,0:T(8,128)(2,1)} %reshape_reshape.3.x_ref), custom_call_target="tpu_custom_call" | custom-call | tf_op jit(solution)/shard_map/pallas_call | solution.py:260
  221.1 1.1 fusion.15
  222.2 0.2 squeeze.14
  222.4 0.2 copy.12
  222.5 1.6 gather_fusion
  224.2 0.0 copy-start.3
  224.2 0.0 copy-start.2
  224.2 0.2 squeeze.15
  224.4 0.0 copy-start.1
  224.4 0.2 copy.13
  224.5 1.6 gather_fusion.1
  226.2 0.0 copy-done.3
  226.2 0.9 broadcast_select_fusion
  227.1 0.0 copy-done.2
  227.1 0.7 copy.16
  227.8 0.0 copy-done.1
  227.8 0.7 copy.17
  (1 shorter events, 0.0 us)
Async XLA Ops:
  0.6 90.7 %copy-start = (bf16[1024,512]{1,0:T(8,128)(2,1)S(1)}, bf16[1024,512]{1,0:T(8,128)(2,1)}, u32[]{:S(2)}) copy-start(bf16[1024,512]{1,0:T(8,128)(2,1)} %param.10) | copy-start | bytes 3145732
  91.3 1.6 copy-start.4
  224.2 2.0 copy-start.3
  224.2 2.9 %copy-start.2 = (f32[128,512]{1,0:T(8,128)S(1)}, f32[128,512]{1,0:T(8,128)}, u32[]{:S(2)}) copy-start(f32[128,512]{1,0:T(8,128)} %get-tuple-element.26) | copy-start | bytes 786436
  224.4 3.4 %copy-start.1 = (f32[128,512]{1,0:T(8,128)S(1)}, f32[128,512]{1,0:T(8,128)}, u32[]{:S(2)}) copy-start(f32[128,512]{1,0:T(8,128)} %get-tuple-element.27) | copy-start | bytes 786436

commit v2 on v1

--- a/solution.py
+++ b/solution.py
@@ -28,7 +28,7 @@
     )
 
 MESH_IDS = pl.DeviceIdType.MESH
-VMEM_LIMIT = 60 * 1024 * 1024
+MIB = 1024 * 1024
 PARTS = 3
 
 
@@ -103,7 +103,7 @@
         out_specs=pl.BlockSpec(memory_space=pltpu.VMEM),
         scratch_shapes=[pltpu.SemaphoreType.DMA((2, PARTS, n - 1)), pltpu.SemaphoreType.DMA((2, PARTS, n - 1))],
         compiler_params=pltpu.CompilerParams(
-            collective_id=0, has_side_effects=True, vmem_limit_bytes=VMEM_LIMIT),
+            collective_id=0, has_side_effects=True, vmem_limit_bytes=16 * MIB),
     )(x)
 
 
@@ -226,7 +226,7 @@
         + [pltpu.VMEM((n_r - 1, block, d_cols), jnp.float32)] * 4
         + [pltpu.SemaphoreType.DMA((2, n_r - 1)), pltpu.SemaphoreType.DMA((2, n_r - 1))],
         compiler_params=pltpu.CompilerParams(
-            collective_id=1, has_side_effects=True, vmem_limit_bytes=VMEM_LIMIT),
+            collective_id=1, has_side_effects=True, vmem_limit_bytes=44 * MIB),
     )(first, second, grad_d, grad_u)
 
 
@@ -264,7 +264,7 @@
         out_specs=pl.BlockSpec(memory_space=pltpu.VMEM),
         scratch_shapes=[pltpu.SemaphoreType.DMA((n_y,)), pltpu.SemaphoreType.DMA((n_y,))],
         compiler_params=pltpu.CompilerParams(
-            collective_id=call_id, has_side_effects=True, vmem_limit_bytes=VMEM_LIMIT),
+            collective_id=call_id, has_side_effects=True, vmem_limit_bytes=8 * MIB),
     )(x)
 
 

time: 229 us -> 204 us (0.89)
  Pallas kernels: 193 us -> 181 us
  local copies, waits for them, and re-layouts: 17 us -> 9.87 us
  matrix products: 15.2 us -> 9.71 us
    pallas_call x1, Pallas kernels: 92.8 us -> 88.1 us  [ring_sum(): pl.pallas_call(functools.partial(ring_sum_kernel, n, n_r), out_shape=(jax...]
    pallas_call x2, Pallas kernels: 41.9 us -> 37.9 us  [y_exchange(): pl.pallas_call(functools.partial(y_exchange_kernel, n_y), out_shape=jax.S...]
    pallas_call x1, Pallas kernels: 58.2 us -> 55.3 us  [ring_gather(): pl.pallas_call(functools.partial(ring_gather_kernel, n), out_shape=jax.Sh...]
    slice x1, local copies, waits for them, and re-layouts: 2.89 us -> 0.51 us  [dispatch(): return (every[0], every[1])]
where the time goes in v2:
time: 204 us
  Pallas kernels  181 us (89%)
  local copies, waits for them, and re-layouts  9.87 us (5%)
  matrix products  9.71 us (5%)
    pallas_call x1, Pallas kernels, ring_sum(): pl.pallas_call(functools.partial(ring_sum_kernel, n, n_r), out_shape=(jax...  88.1 us
    pallas_call x1, Pallas kernels, ring_gather(): pl.pallas_call(functools.partial(ring_gather_kernel, n), out_shape=jax.Sh...  55.3 us
    pallas_call x2, Pallas kernels, y_exchange(): pl.pallas_call(functools.partial(y_exchange_kernel, n_y), out_shape=jax.S...  37.9 us

profile of v2, /device:TPU:6, one launch (start us, length us, event | category | flops | bytes accessed | tf_op | source)
XLA Modules:
  0.0 203.6 jit_solution(9072826796096032561)
XLA Ops:
  0.6 0.0 copy-start
  0.6 0.8 fusion.11
  1.4 1.6 scatter_custom_fusion
  3.1 0.1 stack.7
  3.2 1.6 scatter_custom_fusion.1
  4.8 0.1 stack.8
  5.0 0.1 pad_maximum_fusion.x_ref
  5.0 20.5 %shard_map.93 = bf16[2,8,144,128]{3,2,1,0:T(8,128)(2,1)S(1)} custom-call(bf16[2,8,144,128]{3,2,1,0:T(8,128)(2,1)S(1)} %pad_maximum_fusion.x_ref), custom_call_target="tpu_custom_call" | custom-call | tf_op jit(solution)/shard_map/pallas_call | solution.py:260
  25.5 0.3 reshape.33.x_ref
  25.8 55.3 %shard_map.94 = bf16[2,8,144,1024]{3,2,1,0:T(8,128)(2,1)S(1)} custom-call(bf16[2,144,1024]{2,1,0:T(8,128)(2,1)S(1)} %reshape.33.x_ref), custom_call_target="tpu_custom_call" | custom-call | tf_op jit(solution)/shard_map/pallas_call | solution.py:99
  81.1 0.5 fusion.14
  81.6 0.0 copy-done
  81.6 0.0 copy-start.2
  81.6 1.6 multiply_convert_fusion
  83.2 0.0 copy-done.2
  83.2 2.2 %fusion = bf16[1152,512]{1,0:T(8,128)(2,1)S(1)} fusion(bf16[1152,1024]{1,0:T(8,128)(2,1)S(1)} %bitcast.24, bf16[1024,512]{1,0:T(8,128)(2,1)S(1)} %copy-done.2, f32[1152,512]{1,0:T(8,128)S(1)} %get-tuple-element.19), kind=kOutput, calls=%fused_computation.8 | convolution fusion | flops 1213857792 | bytes 6946816 | tf_op jit(solution)/shard_map/dot_general | solution.py:319
  85.4 1.6 convolution_multiply_fusion.1.gu_ref
  87.0 1.5 convolution_multiply_fusion.2.gd_ref
  88.6 1.4 convolution_convert_fusion
  90.0 1.4 convolution_convert_fusion.1
  91.4 88.1 %shard_map.95 = (bf16[2,144,1024]{2,1,0:T(8,128)(2,1)S(1)}, f32[128,512]{1,0:T(8,128)S(1)}, f32[128,512]{1,0:T(8,128)S(1)}) custom-call(bf16[8,144,1024]{2,1,0:T(8,128)(2,1)S(1)} %bitcast.23, bf16[8,144,1024]{2,1,0:T(8,128)(2,1)S(1)} %bitcast.22, f32[1024,512]{1,0:T(8,128)S(1)} %convolution_multiply_fusion.2.gd_ref, ...), custom_call_target="tpu_custom_call" | custom-call | tf_op jit(solution)/shard_map/pallas_call | solution.py:214
  179.6 0.3 reshape_reshape.3.x_ref
  179.8 17.5 %shard_map.96 = bf16[2,8,144,128]{3,2,1,0:T(8,128)(2,1)S(1)} custom-call(bf16[2,8,144,128]{3,2,1,0:T(8,128)(2,1)S(1)} %reshape_reshape.3.x_ref), custom_call_target="tpu_custom_call" | custom-call | tf_op jit(solution)/shard_map/pallas_call | solution.py:260
  197.3 0.2 squeeze.14
  197.5 0.2 copy.12
  197.7 1.6 gather_fusion
  199.3 0.0 copy-start.1
  199.3 0.2 squeeze.15
  199.5 0.2 copy.13
  199.6 1.6 gather_fusion.1
  201.3 0.0 copy-done.1
  201.3 0.9 broadcast_select_fusion
  202.2 0.7 copy.16
  202.9 0.7 copy.17
  (2 shorter events, 0.0 us)
Async XLA Ops:
  0.6 81.0 %copy-start = (bf16[1024,512]{1,0:T(8,128)(2,1)S(1)}, bf16[1024,512]{1,0:T(8,128)(2,1)}, u32[]{:S(2)}) copy-start(bf16[1024,512]{1,0:T(8,128)(2,1)} %param.10) | copy-start | bytes 3145732
  81.6 1.6 copy-start.2
  199.3 2.0 copy-start.1

commit v3 on v2

--- a/solution.py
+++ b/solution.py
@@ -108,6 +108,7 @@
 
 
 def ring_sum_kernel(n, n_r, pa_ref, pb_ref, gd_ref, gu_ref, o_ref, od_ref, ou_ref, first_r, first_l,
+                    second_out_r, second_out_l, second_r, second_l,
                     send_r, send_l, recv_r, recv_l, send_sem, recv_sem,
                     gsend_f, gsend_b, grecv_f, grecv_b, gsend_sem, grecv_sem):
     pos, rep_at = rep_ring(n_r)
@@ -155,12 +156,16 @@
         return lax.rem(me + 1 + step, n)
 
     firsts = (first_r, first_l)
+    second_outs = (second_out_r, second_out_l)
+    seconds = (second_r, second_l)
 
     def hop(stream, part, step):
         rows = pl.ds(part * half, half)
         if step == 0:
             src = parts[stream].at[chunk_for(stream, 0), rows]
             dst = firsts[stream].at[rows]
+        elif step == 1:
+            src, dst = second_outs[stream].at[rows], seconds[stream].at[rows]
         else:
             src, dst = sends[stream].at[step, rows], recvs[stream].at[step, rows]
         return pltpu.make_async_remote_copy(
@@ -184,12 +189,14 @@
         for stream, part in order:
             rows = pl.ds(part * half, half)
             last[stream, part].wait_recv()
+            here = parts[stream][chunk_for(stream, step), rows].astype(jnp.float32)
             if step == 1:
-                came = firsts[stream][rows].astype(jnp.float32)
+                second_outs[stream][rows] = (
+                    firsts[stream][rows].astype(jnp.float32) + here).astype(second_outs[stream].dtype)
+            elif step == 2:
+                sends[stream][step, rows] = seconds[stream][rows].astype(jnp.float32) + here
             else:
-                came = recvs[stream][step - 1, rows]
-            sends[stream][step, rows] = came + parts[stream][chunk_for(stream, step), rows].astype(
-                jnp.float32)
+                sends[stream][step, rows] = recvs[stream][step - 1, rows] + here
             last[stream, part] = hop(stream, part, step)
             last[stream, part].start()
             copies.append(last[stream, part])
@@ -220,7 +227,7 @@
         ),
         in_specs=[pl.BlockSpec(memory_space=pltpu.VMEM)] * 4,
         out_specs=[pl.BlockSpec(memory_space=pltpu.VMEM)] * 3,
-        scratch_shapes=[pltpu.VMEM((rows, width), first.dtype)] * 2
+        scratch_shapes=[pltpu.VMEM((rows, width), first.dtype)] * 6
         + [pltpu.VMEM((n - 1, rows, width), jnp.float32)] * 4
         + [pltpu.SemaphoreType.DMA((2, PARTS, n - 1)), pltpu.SemaphoreType.DMA((2, PARTS, n - 1))]
         + [pltpu.VMEM((n_r - 1, block, d_cols), jnp.float32)] * 4

time: 204 us -> 198 us (0.971); the launches traced: 204 us -> 195 us
  Pallas kernels: 181 us -> 173 us
    pallas_call x1, Pallas kernels: 88.1 us -> 81.8 us  [ring_sum(): pl.pallas_call(functools.partial(ring_sum_kernel, n, n_r), out_shape=(jax...]
    pallas_call x2, Pallas kernels: 37.9 us -> 35.4 us  [y_exchange(): pl.pallas_call(functools.partial(y_exchange_kernel, n_y), out_shape=jax.S...]
where the time goes in v3:
time: 198 us; the launch traced here: 195 us
  Pallas kernels  173 us (87%)
  local copies, waits for them, and re-layouts  9.87 us (5%)
  matrix products  9.71 us (5%)
    pallas_call x1, Pallas kernels, ring_sum(): pl.pallas_call(functools.partial(ring_sum_kernel, n, n_r), out_shape=(jax...  81.8 us
    pallas_call x1, Pallas kernels, ring_gather(): pl.pallas_call(functools.partial(ring_gather_kernel, n), out_shape=jax.Sh...  55.3 us
    pallas_call x2, Pallas kernels, y_exchange(): pl.pallas_call(functools.partial(y_exchange_kernel, n_y), out_shape=jax.S...  35.4 us

profile of v3, /device:TPU:6, one launch (start us, length us, event | category | flops | bytes accessed | tf_op | source)
XLA Modules:
  0.0 194.7 jit_solution(8231754358535710955)
XLA Ops:
  0.6 0.0 copy-start
  0.6 0.8 fusion.11
  1.4 1.6 scatter_custom_fusion
  3.1 0.1 stack.7
  3.2 1.6 scatter_custom_fusion.1
  4.8 0.1 stack.8
  5.0 0.1 pad_maximum_fusion.x_ref
  5.0 20.5 %shard_map.93 = bf16[2,8,144,128]{3,2,1,0:T(8,128)(2,1)S(1)} custom-call(bf16[2,8,144,128]{3,2,1,0:T(8,128)(2,1)S(1)} %pad_maximum_fusion.x_ref), custom_call_target="tpu_custom_call" | custom-call | tf_op jit(solution)/shard_map/pallas_call | solution.py:267
  25.5 0.3 reshape.33.x_ref
  25.8 55.3 %shard_map.94 = bf16[2,8,144,1024]{3,2,1,0:T(8,128)(2,1)S(1)} custom-call(bf16[2,144,1024]{2,1,0:T(8,128)(2,1)S(1)} %reshape.33.x_ref), custom_call_target="tpu_custom_call" | custom-call | tf_op jit(solution)/shard_map/pallas_call | solution.py:99
  81.1 0.5 fusion.14
  81.6 0.0 copy-done
  81.6 0.0 copy-start.2
  81.6 1.6 multiply_convert_fusion
  83.2 0.0 copy-done.2
  83.2 2.2 %fusion = bf16[1152,512]{1,0:T(8,128)(2,1)S(1)} fusion(bf16[1152,1024]{1,0:T(8,128)(2,1)S(1)} %bitcast.24, bf16[1024,512]{1,0:T(8,128)(2,1)S(1)} %copy-done.2, f32[1152,512]{1,0:T(8,128)S(1)} %get-tuple-element.19), kind=kOutput, calls=%fused_computation.8 | convolution fusion | flops 1213857792 | bytes 6946816 | tf_op jit(solution)/shard_map/dot_general | solution.py:326
  85.4 1.6 convolution_multiply_fusion.1.gu_ref
  87.0 1.5 convolution_multiply_fusion.2.gd_ref
  88.6 1.4 convolution_convert_fusion
  90.0 1.4 convolution_convert_fusion.1
  91.4 81.8 %shard_map.95 = (bf16[2,144,1024]{2,1,0:T(8,128)(2,1)S(1)}, f32[128,512]{1,0:T(8,128)S(1)}, f32[128,512]{1,0:T(8,128)S(1)}) custom-call(bf16[8,144,1024]{2,1,0:T(8,128)(2,1)S(1)} %bitcast.23, bf16[8,144,1024]{2,1,0:T(8,128)(2,1)S(1)} %bitcast.22, f32[1024,512]{1,0:T(8,128)S(1)} %convolution_multiply_fusion.2.gd_ref, ...), custom_call_target="tpu_custom_call" | custom-call | tf_op jit(solution)/shard_map/pallas_call | solution.py:221
  173.2 0.3 reshape_reshape.3.x_ref
  173.5 14.9 %shard_map.96 = bf16[2,8,144,128]{3,2,1,0:T(8,128)(2,1)S(1)} custom-call(bf16[2,8,144,128]{3,2,1,0:T(8,128)(2,1)S(1)} %reshape_reshape.3.x_ref), custom_call_target="tpu_custom_call" | custom-call | tf_op jit(solution)/shard_map/pallas_call | solution.py:267
  188.4 0.2 squeeze.14
  188.6 0.2 copy.12
  188.8 1.6 gather_fusion
  190.4 0.0 copy-start.1
  190.4 0.2 squeeze.15
  190.6 0.2 copy.13
  190.8 1.6 gather_fusion.1
  192.4 0.0 copy-done.1
  192.4 0.9 broadcast_select_fusion
  193.3 0.7 copy.16
  194.0 0.7 copy.17
  (2 shorter events, 0.0 us)
Async XLA Ops:
  0.6 81.0 %copy-start = (bf16[1024,512]{1,0:T(8,128)(2,1)S(1)}, bf16[1024,512]{1,0:T(8,128)(2,1)}, u32[]{:S(2)}) copy-start(bf16[1024,512]{1,0:T(8,128)(2,1)} %param.10) | copy-start | bytes 3145732
  81.6 1.6 copy-start.2
  190.4 2.0 %copy-start.1 = (s32[128]{0:T(128)S(1)}, s32[128]{0:T(128)}, u32[]{:S(2)}) copy-start(s32[128]{0:T(128)} %param.9) | copy-start | bytes 1540

commit v4 on v3

--- a/solution.py
+++ b/solution.py
@@ -285,16 +285,16 @@
 
     def place(values):
         buffer = (
-            jnp.zeros((MODULES * capacity, feature_width), values.dtype)
-            .at[target]
+            jnp.zeros((2, MODULES * capacity, feature_width), values.dtype)
+            .at[:, target]
             .set(values, mode="drop")
         )
-        return buffer.reshape(MODULES, capacity, feature_width)
+        return buffer.reshape(2, MODULES, capacity, feature_width)
 
     n_z = lax.axis_size("lz")
 
     def dispatch(first, second):
-        both = jnp.stack([place(first), place(second)])
+        both = place(jnp.stack([first, second]))
         lanes = 128
         by_y = y_exchange(both.reshape(2, MODULES, -1, lanes), 2)
         every = ring_gather(by_y.reshape(2, -1, feature_width), n_z)
@@ -308,11 +308,11 @@
         summed = summed.reshape(2, -1, capacity, feature_width)
         back = y_exchange(summed.reshape(2, MODULES, -1, 128), 3)
         back = back.reshape(2, MODULES, capacity, feature_width)
-        return back[0], back[1], grad_d, grad_u
+        return back, grad_d, grad_u
 
     def collect(returned):
-        picked = returned[lang_ids, safe_slot]
-        return jnp.where(keep_mask[:, None], picked, jnp.zeros_like(picked))
+        picked = returned[:, lang_ids, safe_slot]
+        return jnp.where(keep_mask[None, :, None], picked, jnp.zeros_like(picked))
 
     flat_tokens, flat_grads = dispatch(tokens, grad_out)
     pre_flat = jnp.dot(flat_tokens, w_up, preferred_element_type=jnp.float32)
@@ -331,8 +331,9 @@
     dx_part = lax.dot_general(
         d_pre, w_up, (((1,), (1,)), ((), ())), preferred_element_type=jnp.float32
     ).astype(jnp.bfloat16)
-    returned, dx_back, grad_down, grad_up = give_back(partial_rows, dx_part, grad_down, grad_up)
-    return (collect(returned), collect(dx_back), grad_up, grad_down)
+    back, grad_down, grad_up = give_back(partial_rows, dx_part, grad_down, grad_up)
+    picked = collect(back)
+    return (picked[0], picked[1], grad_up, grad_down)
 
 
 def solution(mesh):

time: 198 us -> 201 us (1.015)
  local copies, waits for them, and re-layouts: 9.87 us -> 12.4 us
where the time goes in v4:
time: 201 us; the launch traced here: 199 us
  Pallas kernels  174 us (87%)
  local copies, waits for them, and re-layouts  12.4 us (6%)
  matrix products  9.7 us (5%)
  other arithmetic  2.4 us (1%)
    pallas_call x1, Pallas kernels, ring_sum(): pl.pallas_call(functools.partial(ring_sum_kernel, n, n_r), out_shape=(jax...  81.9 us
    pallas_call x1, Pallas kernels, ring_gather(): pl.pallas_call(functools.partial(ring_gather_kernel, n), out_shape=jax.Sh...  55.3 us
    pallas_call x2, Pallas kernels, y_exchange(): pl.pallas_call(functools.partial(y_exchange_kernel, n_y), out_shape=jax.S...  36.5 us
    scatter x2, local copies, waits for them, and re-layouts, place(): buffer = jnp.zeros((2, MODULES * capacity, feature_width), values.dtype)....  4.44 us

profile of v4, /device:TPU:6, one launch (start us, length us, event | category | flops | bytes accessed | tf_op | source)
XLA Modules:
  0.0 199.0 jit_solution(17860592437932270496)
XLA Ops:
  0.6 0.0 copy-start
  0.6 0.8 fusion.8
  1.4 1.1 maximum_bitcast_fusion
  2.5 0.5 copy.15
  3.0 0.3 broadcast_in_dim.29
  3.4 4.3 %scatter_fusion = bf16[2,144,1024]{2,0,1:T(2,128)(2,1)S(1)} fusion(bf16[2,144,1024]{2,0,1:T(2,128)(2,1)S(1)} %broadcast_in_dim.29, s32[128]{0:T(128)S(1)} %get-tuple-element.15, bf16[128,2,1024]{2,1,0:T(2,128)(2,1)S(1)} %copy.15), kind=kCustom, calls=%fused_computation.1 | custom fusion | bytes 1573376 | tf_op jit(solution)/shard_map/scatter | solution.py:290
  7.7 0.1 copy.16
  7.8 0.3 reshape_reshape.6.x_ref
  8.1 20.5 %shard_map.93 = bf16[2,8,144,128]{3,2,1,0:T(8,128)(2,1)S(1)} custom-call(bf16[2,8,144,128]{3,2,1,0:T(8,128)(2,1)S(1)} %reshape_reshape.6.x_ref), custom_call_target="tpu_custom_call" | custom-call | tf_op jit(solution)/shard_map/pallas_call | solution.py:267
  28.6 0.3 reshape.26.x_ref
  28.8 55.3 %shard_map.94 = bf16[2,8,144,1024]{3,2,1,0:T(8,128)(2,1)S(1)} custom-call(bf16[2,144,1024]{2,1,0:T(8,128)(2,1)S(1)} %reshape.26.x_ref), custom_call_target="tpu_custom_call" | custom-call | tf_op jit(solution)/shard_map/pallas_call | solution.py:99
  84.1 0.5 fusion.11
  84.7 0.0 copy-done
  84.7 0.0 copy-start.2
  84.7 1.6 multiply_convert_fusion
  86.3 0.0 copy-done.2
  86.3 2.2 %fusion = bf16[1152,512]{1,0:T(8,128)(2,1)S(1)} fusion(bf16[1152,1024]{1,0:T(8,128)(2,1)S(1)} %bitcast.32, bf16[1024,512]{1,0:T(8,128)(2,1)S(1)} %copy-done.2, f32[1152,512]{1,0:T(8,128)S(1)} %get-tuple-element.17), kind=kOutput, calls=%fused_computation.6 | convolution fusion | flops 1213857792 | bytes 6946816 | tf_op jit(solution)/shard_map/dot_general | solution.py:326
  88.5 1.5 convolution_multiply_fusion.1.gu_ref
  90.0 1.5 convolution_multiply_fusion.2.gd_ref
  91.6 1.4 convolution_convert_fusion
  93.0 1.4 convolution_convert_fusion.1
  94.4 81.9 %shard_map.95 = (bf16[2,144,1024]{2,1,0:T(8,128)(2,1)S(1)}, f32[128,512]{1,0:T(8,128)S(1)}, f32[128,512]{1,0:T(8,128)S(1)}) custom-call(bf16[8,144,1024]{2,1,0:T(8,128)(2,1)S(1)} %bitcast.31, bf16[8,144,1024]{2,1,0:T(8,128)(2,1)S(1)} %bitcast.30, f32[1024,512]{1,0:T(8,128)S(1)} %convolution_multiply_fusion.2.gd_ref, ...), custom_call_target="tpu_custom_call" | custom-call | tf_op jit(solution)/shard_map/pallas_call | solution.py:221
  176.3 0.3 reshape_reshape.7.x_ref
  176.6 0.0 copy-start.1
  176.6 16.0 %shard_map.96 = bf16[2,8,144,128]{3,2,1,0:T(8,128)(2,1)S(1)} custom-call(bf16[2,8,144,128]{3,2,1,0:T(8,128)(2,1)S(1)} %reshape_reshape.7.x_ref), custom_call_target="tpu_custom_call" | custom-call | tf_op jit(solution)/shard_map/pallas_call | solution.py:267
  192.6 0.3 reshape.29
  192.9 0.6 copy.17
  193.5 1.8 gather_fusion
  195.3 0.0 copy-done.1
  195.3 0.5 fusion.5
  195.9 0.7 fusion.12
  196.6 1.0 copy_bitcast_fusion
  197.6 0.7 copy.25
  198.3 0.7 copy.26
  (1 shorter events, 0.0 us)
Async XLA Ops:
  0.6 84.0 %copy-start = (bf16[1024,512]{1,0:T(8,128)(2,1)S(1)}, bf16[1024,512]{1,0:T(8,128)(2,1)}, u32[]{:S(2)}) copy-start(bf16[1024,512]{1,0:T(8,128)(2,1)} %param.10) | copy-start | bytes 3145732
  84.7 1.6 copy-start.2
  176.6 18.7 %copy-start.1 = (s32[128]{0:T(128)S(1)}, s32[128]{0:T(128)}, u32[]{:S(2)}) copy-start(s32[128]{0:T(128)} %param.9) | copy-start | bytes 1540

commit v5 on v2

--- a/solution.py
+++ b/solution.py
@@ -30,6 +30,7 @@
 MESH_IDS = pl.DeviceIdType.MESH
 MIB = 1024 * 1024
 PARTS = 3
+WIDE_FROM = 3
 
 
 def enter(n, others=()):
@@ -108,6 +109,7 @@
 
 
 def ring_sum_kernel(n, n_r, pa_ref, pb_ref, gd_ref, gu_ref, o_ref, od_ref, ou_ref, first_r, first_l,
+                    second_out_r, second_out_l, second_r, second_l,
                     send_r, send_l, recv_r, recv_l, send_sem, recv_sem,
                     gsend_f, gsend_b, grecv_f, grecv_b, gsend_sem, grecv_sem):
     pos, rep_at = rep_ring(n_r)
@@ -155,12 +157,17 @@
         return lax.rem(me + 1 + step, n)
 
     firsts = (first_r, first_l)
+    second_outs = (second_out_r, second_out_l)
+    seconds = (second_r, second_l)
 
     def hop(stream, part, step):
         rows = pl.ds(part * half, half)
         if step == 0:
             src = parts[stream].at[chunk_for(stream, 0), rows]
             dst = firsts[stream].at[rows]
+        elif step < WIDE_FROM:
+            src = second_outs[stream].at[step - 1, rows]
+            dst = seconds[stream].at[step - 1, rows]
         else:
             src, dst = sends[stream].at[step, rows], recvs[stream].at[step, rows]
         return pltpu.make_async_remote_copy(
@@ -184,12 +191,17 @@
         for stream, part in order:
             rows = pl.ds(part * half, half)
             last[stream, part].wait_recv()
+            here = parts[stream][chunk_for(stream, step), rows].astype(jnp.float32)
             if step == 1:
                 came = firsts[stream][rows].astype(jnp.float32)
+            elif step <= WIDE_FROM:
+                came = seconds[stream][step - 2, rows].astype(jnp.float32)
             else:
                 came = recvs[stream][step - 1, rows]
-            sends[stream][step, rows] = came + parts[stream][chunk_for(stream, step), rows].astype(
-                jnp.float32)
+            if step < WIDE_FROM:
+                second_outs[stream][step - 1, rows] = (came + here).astype(second_outs[stream].dtype)
+            else:
+                sends[stream][step, rows] = came + here
             last[stream, part] = hop(stream, part, step)
             last[stream, part].start()
             copies.append(last[stream, part])
@@ -221,6 +233,7 @@
         in_specs=[pl.BlockSpec(memory_space=pltpu.VMEM)] * 4,
         out_specs=[pl.BlockSpec(memory_space=pltpu.VMEM)] * 3,
         scratch_shapes=[pltpu.VMEM((rows, width), first.dtype)] * 2
+        + [pltpu.VMEM((WIDE_FROM - 1, rows, width), first.dtype)] * 4
         + [pltpu.VMEM((n - 1, rows, width), jnp.float32)] * 4
         + [pltpu.SemaphoreType.DMA((2, PARTS, n - 1)), pltpu.SemaphoreType.DMA((2, PARTS, n - 1))]
         + [pltpu.VMEM((n_r - 1, block, d_cols), jnp.float32)] * 4

time: 204 us -> 191 us (0.936)
  Pallas kernels: 181 us -> 168 us
    pallas_call x1, Pallas kernels: 88.1 us -> 76.9 us  [ring_sum(): pl.pallas_call(functools.partial(ring_sum_kernel, n, n_r), out_shape=(jax...]
where the time goes in v5:
time: 191 us
  Pallas kernels  168 us (88%)
  local copies, waits for them, and re-layouts  9.87 us (5%)
  matrix products  9.71 us (5%)
    pallas_call x1, Pallas kernels, ring_sum(): pl.pallas_call(functools.partial(ring_sum_kernel, n, n_r), out_shape=(jax...  76.9 us
    pallas_call x1, Pallas kernels, ring_gather(): pl.pallas_call(functools.partial(ring_gather_kernel, n), out_shape=jax.Sh...  55.3 us
    pallas_call x2, Pallas kernels, y_exchange(): pl.pallas_call(functools.partial(y_exchange_kernel, n_y), out_shape=jax.S...  36.2 us

profile of v5, /device:TPU:6, one launch (start us, length us, event | category | flops | bytes accessed | tf_op | source)
XLA Modules:
  0.0 190.6 jit_solution(756912199463445198)
XLA Ops:
  0.6 0.0 copy-start
  0.6 0.8 fusion.11
  1.4 1.6 scatter_custom_fusion
  3.1 0.1 stack.7
  3.2 1.6 scatter_custom_fusion.1
  4.8 0.1 stack.8
  5.0 0.1 pad_maximum_fusion.x_ref
  5.0 20.5 %shard_map.93 = bf16[2,8,144,128]{3,2,1,0:T(8,128)(2,1)S(1)} custom-call(bf16[2,8,144,128]{3,2,1,0:T(8,128)(2,1)S(1)} %pad_maximum_fusion.x_ref), custom_call_target="tpu_custom_call" | custom-call | tf_op jit(solution)/shard_map/pallas_call | solution.py:273
  25.5 0.3 reshape.33.x_ref
  25.8 55.3 %shard_map.94 = bf16[2,8,144,1024]{3,2,1,0:T(8,128)(2,1)S(1)} custom-call(bf16[2,144,1024]{2,1,0:T(8,128)(2,1)S(1)} %reshape.33.x_ref), custom_call_target="tpu_custom_call" | custom-call | tf_op jit(solution)/shard_map/pallas_call | solution.py:100
  81.1 0.5 fusion.14
  81.6 0.0 copy-done
  81.6 0.0 copy-start.2
  81.6 1.6 multiply_convert_fusion
  83.2 0.0 copy-done.2
  83.2 2.2 %fusion = bf16[1152,512]{1,0:T(8,128)(2,1)S(1)} fusion(bf16[1152,1024]{1,0:T(8,128)(2,1)S(1)} %bitcast.24, bf16[1024,512]{1,0:T(8,128)(2,1)S(1)} %copy-done.2, f32[1152,512]{1,0:T(8,128)S(1)} %get-tuple-element.19), kind=kOutput, calls=%fused_computation.8 | convolution fusion | flops 1213857792 | bytes 6946816 | tf_op jit(solution)/shard_map/dot_general | solution.py:332
  85.4 1.6 convolution_multiply_fusion.1.gu_ref
  87.0 1.5 convolution_multiply_fusion.2.gd_ref
  88.6 1.4 convolution_convert_fusion
  90.0 1.4 convolution_convert_fusion.1
  91.4 76.9 %shard_map.95 = (bf16[2,144,1024]{2,1,0:T(8,128)(2,1)S(1)}, f32[128,512]{1,0:T(8,128)S(1)}, f32[128,512]{1,0:T(8,128)S(1)}) custom-call(bf16[8,144,1024]{2,1,0:T(8,128)(2,1)S(1)} %bitcast.23, bf16[8,144,1024]{2,1,0:T(8,128)(2,1)S(1)} %bitcast.22, f32[1024,512]{1,0:T(8,128)S(1)} %convolution_multiply_fusion.2.gd_ref, ...), custom_call_target="tpu_custom_call" | custom-call | tf_op jit(solution)/shard_map/pallas_call | solution.py:226
  168.3 0.3 reshape_reshape.3.x_ref
  168.5 15.8 %shard_map.96 = bf16[2,8,144,128]{3,2,1,0:T(8,128)(2,1)S(1)} custom-call(bf16[2,8,144,128]{3,2,1,0:T(8,128)(2,1)S(1)} %reshape_reshape.3.x_ref), custom_call_target="tpu_custom_call" | custom-call | tf_op jit(solution)/shard_map/pallas_call | solution.py:273
  184.4 0.2 squeeze.14
  184.5 0.2 copy.12
  184.7 1.6 gather_fusion
  186.3 0.0 copy-start.1
  186.3 0.2 squeeze.15
  186.5 0.2 copy.13
  186.7 1.6 gather_fusion.1
  188.3 0.0 copy-done.1
  188.3 0.9 broadcast_select_fusion
  189.2 0.7 copy.16
  189.9 0.7 copy.17
  (2 shorter events, 0.0 us)
Async XLA Ops:
  0.6 81.0 %copy-start = (bf16[1024,512]{1,0:T(8,128)(2,1)S(1)}, bf16[1024,512]{1,0:T(8,128)(2,1)}, u32[]{:S(2)}) copy-start(bf16[1024,512]{1,0:T(8,128)(2,1)} %param.10) | copy-start | bytes 3145732
  81.6 1.6 copy-start.2
  186.3 2.0 %copy-start.1 = (s32[128]{0:T(128)S(1)}, s32[128]{0:T(128)}, u32[]{:S(2)}) copy-start(s32[128]{0:T(128)} %param.9) | copy-start | bytes 1540

commit v6 on v5

--- a/solution.py
+++ b/solution.py
@@ -58,51 +58,66 @@
     return pos, rep_at
 
 
-def ring_gather_kernel(n, x_ref, o_ref, send_sem, recv_sem):
-    me, right, left = enter(n)
-    half = x_ref.shape[1] // PARTS
-    o_ref[0, me] = x_ref[0]
-    o_ref[1, me] = x_ref[1]
-
-    def hop(stream, part, step):
-        rows = pl.ds(part * half, half)
+def ring_gather_kernel(n, x_ref, o_ref, send_sem, recv_sem, y_send, y_recv):
+    n_y = x_ref.shape[1]
+    me_y = lax.axis_index("ly")
+    ys = [("ly", lax.rem(me_y + k, n_y)) for k in range(1, n_y)]
+    me, right, left = enter(n, ys)
+
+    def y_hop(k, src, dst):
+        return pltpu.make_async_remote_copy(
+            src_ref=src, dst_ref=dst, send_sem=y_send.at[k], recv_sem=y_recv.at[k],
+            device_id={"ly": lax.rem(me_y + k, n_y)}, device_id_type=MESH_IDS)
+
+    y_copies = []
+    for k in range(1, n_y):
+        copy = y_hop(k, x_ref.at[:, lax.rem(me_y + k, n_y)], o_ref.at[:, me, me_y])
+        copy.start()
+        y_copies.append(copy)
+    o_ref[:, me, me_y] = x_ref[:, me_y]
+
+    def hop(stream, k, step):
+        source = lax.rem(me_y + n_y - k, n_y)
         if stream == 0:
             slot, peer = lax.rem(me - step + n, n), right
         else:
             slot, peer = lax.rem(me + step, n), left
-        src = x_ref.at[stream, rows] if step == 0 else o_ref.at[stream, slot, rows]
-        return pltpu.make_async_remote_copy(
-            src_ref=src, dst_ref=o_ref.at[stream, slot, rows],
-            send_sem=send_sem.at[stream, part, step], recv_sem=recv_sem.at[stream, part, step],
+        return pltpu.make_async_remote_copy(
+            src_ref=o_ref.at[stream, slot, source], dst_ref=o_ref.at[stream, slot, source],
+            send_sem=send_sem.at[stream, k, step], recv_sem=recv_sem.at[stream, k, step],
             device_id={"lz": peer}, device_id_type=MESH_IDS)
 
-    order = [(stream, part) for part in range(PARTS) for stream in range(2)]
     copies = []
     last = {}
-    for key in order:
-        last[key] = hop(*key, 0)
-        last[key].start()
-        copies.append(last[key])
+    for k in range(n_y):
+        if k > 0:
+            y_hop(k, x_ref.at[:, me_y], o_ref.at[:, me, lax.rem(me_y + n_y - k, n_y)]).wait_recv()
+        for stream in range(2):
+            last[stream, k] = hop(stream, k, 0)
+            last[stream, k].start()
+            copies.append(last[stream, k])
     for step in range(1, n - 1):
-        for key in order:
-            last[key].wait_recv()
-            last[key] = hop(*key, step)
-            last[key].start()
-            copies.append(last[key])
-    for key in order:
+        for k in range(n_y):
+            for stream in range(2):
+                last[stream, k].wait_recv()
+                last[stream, k] = hop(stream, k, step)
+                last[stream, k].start()
+                copies.append(last[stream, k])
+    for key in last:
         last[key].wait_recv()
-    for copy in copies:
+    for copy in copies + y_copies:
         copy.wait_send()
 
 
 def ring_gather(x, n):
-    two, rows, width = x.shape
+    two, n_y, rows, lanes = x.shape
     return pl.pallas_call(
         functools.partial(ring_gather_kernel, n),
-        out_shape=jax.ShapeDtypeStruct((two, n, rows, width), x.dtype),
+        out_shape=jax.ShapeDtypeStruct((two, n, n_y, rows, lanes), x.dtype),
         in_specs=[pl.BlockSpec(memory_space=pltpu.VMEM)],
         out_specs=pl.BlockSpec(memory_space=pltpu.VMEM),
-        scratch_shapes=[pltpu.SemaphoreType.DMA((2, PARTS, n - 1)), pltpu.SemaphoreType.DMA((2, PARTS, n - 1))],
+        scratch_shapes=[pltpu.SemaphoreType.DMA((2, n_y, n - 1)), pltpu.SemaphoreType.DMA((2, n_y, n - 1)),
+                        pltpu.SemaphoreType.DMA((n_y,)), pltpu.SemaphoreType.DMA((n_y,))],
         compiler_params=pltpu.CompilerParams(
             collective_id=0, has_side_effects=True, vmem_limit_bytes=16 * MIB),
     )(x)
@@ -302,8 +317,7 @@
     def dispatch(first, second):
         both = jnp.stack([place(first), place(second)])
         lanes = 128
-        by_y = y_exchange(both.reshape(2, MODULES, -1, lanes), 2)
-        every = ring_gather(by_y.reshape(2, -1, feature_width), n_z)
+        every = ring_gather(both.reshape(2, MODULES, -1, lanes), n_z)
         every = every.reshape(2, -1, feature_width)
         return every[0], every[1]
 

time: 191 us -> 200 us (1.047)
  local copies, waits for them, and re-layouts: 9.87 us -> 18.3 us
  Pallas kernels: 168 us -> 165 us
    pallas_call x2 -> x1, Pallas kernels: 36.2 us -> 18.3 us  [y_exchange(): pl.pallas_call(functools.partial(y_exchange_kernel, n_y), out_shape=jax.S...]
    pallas_call x1, Pallas kernels: 55.3 us -> 72.2 us  [ring_gather(): pl.pallas_call(functools.partial(ring_gather_kernel, n), out_shape=jax.Sh...]
    squeeze x0 -> x2, local copies, waits for them, and re-layouts: none -> 7.35 us  [dispatch(): return (every[0], every[1])]
    pallas_call x1, Pallas kernels: 76.9 us -> 74.5 us  [ring_sum(): pl.pallas_call(functools.partial(ring_sum_kernel, n, n_r), out_shape=(jax...]
where the time goes in v6:
time: 200 us; the launch traced here: 198 us
  Pallas kernels  165 us (82%)
  local copies, waits for them, and re-layouts  18.3 us (9%)
  matrix products  11.6 us (6%)
  other arithmetic  2.38 us (1%)
    pallas_call x1, Pallas kernels, ring_sum(): pl.pallas_call(functools.partial(ring_sum_kernel, n, n_r), out_shape=(jax...  74.5 us
    pallas_call x1, Pallas kernels, ring_gather(): pl.pallas_call(functools.partial(ring_gather_kernel, n), out_shape=jax.Sh...  72.2 us
    pallas_call x1, Pallas kernels, y_exchange(): pl.pallas_call(functools.partial(y_exchange_kernel, n_y), out_shape=jax.S...  18.3 us
    squeeze x2, local copies, waits for them, and re-layouts, dispatch(): return (every[0], every[1])  7.35 us

profile of v6, /device:TPU:6, one launch (start us, length us, event | category | flops | bytes accessed | tf_op | source)
XLA Modules:
  0.0 198.1 jit_solution(5668097901741194150)
XLA Ops:
  0.6 0.0 copy-start
  0.6 0.7 broadcast_compare_fusion
  1.4 0.7 fusion.11
  2.1 1.6 scatter_custom_fusion
  3.7 0.1 stack.7
  3.8 1.6 scatter_custom_fusion.1
  5.5 0.1 stack.8
  5.6 0.1 pad_maximum_fusion.x_ref
  5.7 72.2 %shard_map.93 = bf16[2,8,8,144,128]{4,3,2,1,0:T(8,128)(2,1)S(1)} custom-call(bf16[2,8,144,128]{3,2,1,0:T(8,128)(2,1)S(1)} %pad_maximum_fusion.x_ref), custom_call_target="tpu_custom_call" | custom-call | tf_op jit(solution)/shard_map/pallas_call | solution.py:114
  77.9 1.7 fusion.14
  79.6 4.9 %squeeze.13 = bf16[1152,1024]{1,0:T(8,128)(2,1)} reshape(bf16[1,8,8,144,128]{4,3,2,1,0:T(8,128)(2,1)} %get-tuple-element.10) | data formatting | bytes 4718592 | tf_op jit(solution)/shard_map/squeeze | solution.py:322
  84.6 2.4 %squeeze.12 = bf16[1152,1024]{1,0:T(8,128)(2,1)} reshape(bf16[1,8,8,144,128]{4,3,2,1,0:T(8,128)(2,1)S(1)} %get-tuple-element.11) | data formatting | bytes 4718592 | tf_op jit(solution)/shard_map/squeeze | solution.py:322
  87.0 0.0 copy-done
  87.0 0.0 copy-start.1
  87.0 0.0 copy-start.3
  87.0 3.4 %multiply_convert_fusion = (bf16[1152,512]{1,0:T(8,128)(2,1)S(1)}, f32[1152,512]{1,0:T(8,128)S(1)}) fusion(bf16[1152,1024]{1,0:T(8,128)(2,1)} %squeeze.12, bf16[1024,512]{1,0:T(8,128)(2,1)S(1)} %copy-done), kind=kOutput, calls=%fused_computation.13 | convolution fusion | flops 1210908672 | bytes 6946816 | tf_op jit(solution)/shard_map/dot_general | solution.py:338
  90.4 0.0 copy-done.1
  90.4 0.0 copy-done.3
  90.4 2.2 %fusion = bf16[1152,512]{1,0:T(8,128)(2,1)S(1)} fusion(bf16[1152,1024]{1,0:T(8,128)(2,1)S(1)} %copy-done.1, bf16[1024,512]{1,0:T(8,128)(2,1)S(1)} %copy-done.3, f32[1152,512]{1,0:T(8,128)S(1)} %get-tuple-element.19), kind=kOutput, calls=%fused_computation.8 | convolution fusion | flops 1213857792 | bytes 6946816 | tf_op jit(solution)/shard_map/dot_general | solution.py:346
  92.7 0.0 copy-start.2
  92.7 1.5 convolution_multiply_fusion.2.gd_ref
  94.2 0.1 copy-done.2
  94.3 1.6 convolution_multiply_fusion.1.gu_ref
  95.9 1.4 convolution_convert_fusion
  97.3 1.4 convolution_convert_fusion.1
  98.8 74.5 %shard_map.94 = (bf16[2,144,1024]{2,1,0:T(8,128)(2,1)S(1)}, f32[128,512]{1,0:T(8,128)S(1)}, f32[128,512]{1,0:T(8,128)S(1)}) custom-call(bf16[8,144,1024]{2,1,0:T(8,128)(2,1)S(1)} %bitcast.25, bf16[8,144,1024]{2,1,0:T(8,128)(2,1)S(1)} %bitcast.24, f32[1024,512]{1,0:T(8,128)S(1)} %convolution_multiply_fusion.2.gd_ref, ...), custom_call_target="tpu_custom_call" | custom-call | tf_op jit(solution)/shard_map/pallas_call | solution.py:241
  173.2 0.3 reshape_reshape.3.x_ref
  173.5 18.3 %shard_map.95 = bf16[2,8,144,128]{3,2,1,0:T(8,128)(2,1)S(1)} custom-call(bf16[2,8,144,128]{3,2,1,0:T(8,128)(2,1)S(1)} %reshape_reshape.3.x_ref), custom_call_target="tpu_custom_call" | custom-call | tf_op jit(solution)/shard_map/pallas_call | solution.py:288
  191.9 0.2 squeeze.15
  192.1 0.2 copy.13
  192.2 1.6 gather_fusion.1
  193.9 0.2 squeeze.14
  194.0 0.2 copy.12
  194.2 1.6 gather_fusion
  195.8 0.9 broadcast_select_fusion
  196.7 0.7 copy.16
  197.4 0.7 copy.17
  (1 shorter events, 0.0 us)
Async XLA Ops:
  0.6 86.4 %copy-start = (bf16[1024,512]{1,0:T(8,128)(2,1)S(1)}, bf16[1024,512]{1,0:T(8,128)(2,1)}, u32[]{:S(2)}) copy-start(bf16[1024,512]{1,0:T(8,128)(2,1)} %param.10) | copy-start | bytes 3145732
  87.0 3.4 %copy-start.1 = (bf16[1152,1024]{1,0:T(8,128)(2,1)S(1)}, bf16[1152,1024]{1,0:T(8,128)(2,1)}, u32[]{:S(2)}) copy-start(bf16[1152,1024]{1,0:T(8,128)(2,1)} %squeeze.13) | copy-start | bytes 7077892
  87.0 3.4 %copy-start.3 = (bf16[1024,512]{1,0:T(8,128)(2,1)S(1)}, bf16[1024,512]{1,0:T(8,128)(2,1)}, u32[]{:S(2)}) copy-start(bf16[1024,512]{1,0:T(8,128)(2,1)} %param.11) | copy-start | bytes 3145732
  92.7 1.7 copy-start.2

commit v7 on v5

--- a/solution.py
+++ b/solution.py
@@ -30,7 +30,7 @@
 MESH_IDS = pl.DeviceIdType.MESH
 MIB = 1024 * 1024
 PARTS = 3
-WIDE_FROM = 3
+WIDE_FROM = 4
 
 
 def enter(n, others=()):

time: 191 us -> 186 us (0.974)
  Pallas kernels: 168 us -> 163 us
    pallas_call x1, Pallas kernels: 76.9 us -> 70.9 us  [ring_sum(): pl.pallas_call(functools.partial(ring_sum_kernel, n, n_r), out_shape=(jax...]
where the time goes in v7:
time: 186 us; the launch traced here: 185 us
  Pallas kernels  163 us (88%)
  local copies, waits for them, and re-layouts  9.87 us (5%)
  matrix products  9.71 us (5%)
    pallas_call x1, Pallas kernels, ring_sum(): pl.pallas_call(functools.partial(ring_sum_kernel, n, n_r), out_shape=(jax...  70.9 us
    pallas_call x1, Pallas kernels, ring_gather(): pl.pallas_call(functools.partial(ring_gather_kernel, n), out_shape=jax.Sh...  55.3 us
    pallas_call x2, Pallas kernels, y_exchange(): pl.pallas_call(functools.partial(y_exchange_kernel, n_y), out_shape=jax.S...  37.1 us

profile of v7, /device:TPU:6, one launch (start us, length us, event | category | flops | bytes accessed | tf_op | source)
XLA Modules:
  0.0 185.5 jit_solution(5167856783110519640)
XLA Ops:
  0.6 0.0 copy-start
  0.6 0.8 fusion.11
  1.4 1.6 scatter_custom_fusion
  3.1 0.1 stack.7
  3.2 1.6 scatter_custom_fusion.1
  4.8 0.1 stack.8
  5.0 0.1 pad_maximum_fusion.x_ref
  5.0 20.5 %shard_map.93 = bf16[2,8,144,128]{3,2,1,0:T(8,128)(2,1)S(1)} custom-call(bf16[2,8,144,128]{3,2,1,0:T(8,128)(2,1)S(1)} %pad_maximum_fusion.x_ref), custom_call_target="tpu_custom_call" | custom-call | tf_op jit(solution)/shard_map/pallas_call | solution.py:273
  25.5 0.3 reshape.33.x_ref
  25.8 55.3 %shard_map.94 = bf16[2,8,144,1024]{3,2,1,0:T(8,128)(2,1)S(1)} custom-call(bf16[2,144,1024]{2,1,0:T(8,128)(2,1)S(1)} %reshape.33.x_ref), custom_call_target="tpu_custom_call" | custom-call | tf_op jit(solution)/shard_map/pallas_call | solution.py:100
  81.1 0.5 fusion.14
  81.6 0.0 copy-done
  81.6 0.0 copy-start.2
  81.6 1.6 multiply_convert_fusion
  83.2 0.0 copy-done.2
  83.2 2.2 %fusion = bf16[1152,512]{1,0:T(8,128)(2,1)S(1)} fusion(bf16[1152,1024]{1,0:T(8,128)(2,1)S(1)} %bitcast.24, bf16[1024,512]{1,0:T(8,128)(2,1)S(1)} %copy-done.2, f32[1152,512]{1,0:T(8,128)S(1)} %get-tuple-element.19), kind=kOutput, calls=%fused_computation.8 | convolution fusion | flops 1213857792 | bytes 6946816 | tf_op jit(solution)/shard_map/dot_general | solution.py:332
  85.4 1.6 convolution_multiply_fusion.1.gu_ref
  87.0 1.5 convolution_multiply_fusion.2.gd_ref
  88.6 1.4 convolution_convert_fusion
  90.0 1.4 convolution_convert_fusion.1
  91.4 70.9 %shard_map.95 = (bf16[2,144,1024]{2,1,0:T(8,128)(2,1)S(1)}, f32[128,512]{1,0:T(8,128)S(1)}, f32[128,512]{1,0:T(8,128)S(1)}) custom-call(bf16[8,144,1024]{2,1,0:T(8,128)(2,1)S(1)} %bitcast.23, bf16[8,144,1024]{2,1,0:T(8,128)(2,1)S(1)} %bitcast.22, f32[1024,512]{1,0:T(8,128)S(1)} %convolution_multiply_fusion.2.gd_ref, ...), custom_call_target="tpu_custom_call" | custom-call | tf_op jit(solution)/shard_map/pallas_call | solution.py:226
  162.3 0.3 reshape_reshape.3.x_ref
  162.6 16.6 %shard_map.96 = bf16[2,8,144,128]{3,2,1,0:T(8,128)(2,1)S(1)} custom-call(bf16[2,8,144,128]{3,2,1,0:T(8,128)(2,1)S(1)} %reshape_reshape.3.x_ref), custom_call_target="tpu_custom_call" | custom-call | tf_op jit(solution)/shard_map/pallas_call | solution.py:273
  179.2 0.2 squeeze.14
  179.4 0.2 copy.12
  179.6 1.6 gather_fusion
  181.2 0.0 copy-start.1
  181.2 0.2 squeeze.15
  181.4 0.2 copy.13
  181.5 1.6 gather_fusion.1
  183.2 0.0 copy-done.1
  183.2 0.9 broadcast_select_fusion
  184.1 0.7 copy.16
  184.8 0.7 copy.17
  (2 shorter events, 0.0 us)
Async XLA Ops:
  0.6 81.0 %copy-start = (bf16[1024,512]{1,0:T(8,128)(2,1)S(1)}, bf16[1024,512]{1,0:T(8,128)(2,1)}, u32[]{:S(2)}) copy-start(bf16[1024,512]{1,0:T(8,128)(2,1)} %param.10) | copy-start | bytes 3145732
  81.6 1.6 copy-start.2
  181.2 2.0 %copy-start.1 = (s32[128]{0:T(128)S(1)}, s32[128]{0:T(128)}, u32[]{:S(2)}) copy-start(s32[128]{0:T(128)} %param.9) | copy-start | bytes 1540

commit v8 on v7

--- a/solution.py
+++ b/solution.py
@@ -184,9 +184,9 @@
         copies.append(last[stream, part])
     grad_step(0)
     for step in range(1, max(n, n_r) - 1):
-        if step < n_r - 1:
-            grad_step(step)
         if step >= n - 1:
+            if step < n_r - 1:
+                grad_step(step)
             continue
         for stream, part in order:
             rows = pl.ds(part * half, half)
@@ -205,6 +205,8 @@
             last[stream, part] = hop(stream, part, step)
             last[stream, part].start()
             copies.append(last[stream, part])
+        if step < n_r - 1:
+            grad_step(step)
     for stream, part in order:
         rows = pl.ds(part * half, half)
         last[stream, part].wait_recv()

time: 186 us -> 186 us (level)
  no operation moved by 1% of the time
where the time goes in v8:
time: 186 us; the launch traced here: 185 us
  Pallas kernels  163 us (88%)
  local copies, waits for them, and re-layouts  9.87 us (5%)
  matrix products  9.71 us (5%)
    pallas_call x1, Pallas kernels, ring_sum(): pl.pallas_call(functools.partial(ring_sum_kernel, n, n_r), out_shape=(jax...  69.2 us
    pallas_call x1, Pallas kernels, ring_gather(): pl.pallas_call(functools.partial(ring_gather_kernel, n), out_shape=jax.Sh...  55.3 us
    pallas_call x2, Pallas kernels, y_exchange(): pl.pallas_call(functools.partial(y_exchange_kernel, n_y), out_shape=jax.S...  38.3 us

profile of v8, /device:TPU:6, one launch (start us, length us, event | category | flops | bytes accessed | tf_op | source)
XLA Modules:
  0.0 185.0 jit_solution(14726564389968912208)
XLA Ops:
  0.6 0.0 copy-start
  0.6 0.8 fusion.11
  1.4 1.6 scatter_custom_fusion
  3.1 0.1 stack.7
  3.2 1.6 scatter_custom_fusion.1
  4.8 0.1 stack.8
  5.0 0.1 pad_maximum_fusion.x_ref
  5.0 20.5 %shard_map.93 = bf16[2,8,144,128]{3,2,1,0:T(8,128)(2,1)S(1)} custom-call(bf16[2,8,144,128]{3,2,1,0:T(8,128)(2,1)S(1)} %pad_maximum_fusion.x_ref), custom_call_target="tpu_custom_call" | custom-call | tf_op jit(solution)/shard_map/pallas_call | solution.py:275
  25.5 0.3 reshape.33.x_ref
  25.8 55.3 %shard_map.94 = bf16[2,8,144,1024]{3,2,1,0:T(8,128)(2,1)S(1)} custom-call(bf16[2,144,1024]{2,1,0:T(8,128)(2,1)S(1)} %reshape.33.x_ref), custom_call_target="tpu_custom_call" | custom-call | tf_op jit(solution)/shard_map/pallas_call | solution.py:100
  81.1 0.5 fusion.14
  81.6 0.0 copy-done
  81.6 0.0 copy-start.2
  81.6 1.6 multiply_convert_fusion
  83.2 0.0 copy-done.2
  83.2 2.2 %fusion = bf16[1152,512]{1,0:T(8,128)(2,1)S(1)} fusion(bf16[1152,1024]{1,0:T(8,128)(2,1)S(1)} %bitcast.24, bf16[1024,512]{1,0:T(8,128)(2,1)S(1)} %copy-done.2, f32[1152,512]{1,0:T(8,128)S(1)} %get-tuple-element.19), kind=kOutput, calls=%fused_computation.8 | convolution fusion | flops 1213857792 | bytes 6946816 | tf_op jit(solution)/shard_map/dot_general | solution.py:334
  85.4 1.6 convolution_multiply_fusion.1.gu_ref
  87.0 1.5 convolution_multiply_fusion.2.gd_ref
  88.6 1.4 convolution_convert_fusion
  90.0 1.4 convolution_convert_fusion.1
  91.4 69.2 %shard_map.95 = (bf16[2,144,1024]{2,1,0:T(8,128)(2,1)S(1)}, f32[128,512]{1,0:T(8,128)S(1)}, f32[128,512]{1,0:T(8,128)S(1)}) custom-call(bf16[8,144,1024]{2,1,0:T(8,128)(2,1)S(1)} %bitcast.23, bf16[8,144,1024]{2,1,0:T(8,128)(2,1)S(1)} %bitcast.22, f32[1024,512]{1,0:T(8,128)S(1)} %convolution_multiply_fusion.2.gd_ref, ...), custom_call_target="tpu_custom_call" | custom-call | tf_op jit(solution)/shard_map/pallas_call | solution.py:228
  160.6 0.3 reshape_reshape.3.x_ref
  160.9 17.8 %shard_map.96 = bf16[2,8,144,128]{3,2,1,0:T(8,128)(2,1)S(1)} custom-call(bf16[2,8,144,128]{3,2,1,0:T(8,128)(2,1)S(1)} %reshape_reshape.3.x_ref), custom_call_target="tpu_custom_call" | custom-call | tf_op jit(solution)/shard_map/pallas_call | solution.py:275
  178.7 0.2 squeeze.14
  178.9 0.2 copy.12
  179.0 1.6 gather_fusion
  180.7 0.0 copy-start.1
  180.7 0.2 squeeze.15
  180.8 0.2 copy.13
  181.0 1.6 gather_fusion.1
  182.6 0.0 copy-done.1
  182.7 0.9 broadcast_select_fusion
  183.6 0.7 copy.16
  184.3 0.7 copy.17
  (2 shorter events, 0.0 us)
Async XLA Ops:
  0.6 81.0 %copy-start = (bf16[1024,512]{1,0:T(8,128)(2,1)S(1)}, bf16[1024,512]{1,0:T(8,128)(2,1)}, u32[]{:S(2)}) copy-start(bf16[1024,512]{1,0:T(8,128)(2,1)} %param.10) | copy-start | bytes 3145732
  81.6 1.6 copy-start.2
  180.7 2.0 %copy-start.1 = (s32[128]{0:T(128)S(1)}, s32[128]{0:T(128)}, u32[]{:S(2)}) copy-start(s32[128]{0:T(128)} %param.9) | copy-start | bytes 1540

commit v9 on v8

--- a/solution.py
+++ b/solution.py
@@ -61,8 +61,6 @@
 def ring_gather_kernel(n, x_ref, o_ref, send_sem, recv_sem):
     me, right, left = enter(n)
     half = x_ref.shape[1] // PARTS
-    o_ref[0, me] = x_ref[0]
-    o_ref[1, me] = x_ref[1]
 
     def hop(stream, part, step):
         rows = pl.ds(part * half, half)
@@ -83,6 +81,8 @@
         last[key] = hop(*key, 0)
         last[key].start()
         copies.append(last[key])
+    o_ref[0, me] = x_ref[0]
+    o_ref[1, me] = x_ref[1]
     for step in range(1, n - 1):
         for key in order:
             last[key].wait_recv()

time: 186 us -> 186 us (level)
  no operation moved by 1% of the time
where the time goes in v9:
time: 186 us; the launch traced here: 185 us
  Pallas kernels  163 us (88%)
  local copies, waits for them, and re-layouts  9.87 us (5%)
  matrix products  9.7 us (5%)
    pallas_call x1, Pallas kernels, ring_sum(): pl.pallas_call(functools.partial(ring_sum_kernel, n, n_r), out_shape=(jax...  69.2 us
    pallas_call x1, Pallas kernels, ring_gather(): pl.pallas_call(functools.partial(ring_gather_kernel, n), out_shape=jax.Sh...  55.3 us
    pallas_call x2, Pallas kernels, y_exchange(): pl.pallas_call(functools.partial(y_exchange_kernel, n_y), out_shape=jax.S...  38.2 us

profile of v9, /device:TPU:6, one launch (start us, length us, event | category | flops | bytes accessed | tf_op | source)
XLA Modules:
  0.0 184.9 jit_solution(5830529907063121905)
XLA Ops:
  0.6 0.0 copy-start
  0.6 0.8 fusion.11
  1.4 1.6 scatter_custom_fusion
  3.1 0.1 stack.7
  3.2 1.6 scatter_custom_fusion.1
  4.8 0.1 stack.8
  5.0 0.1 pad_maximum_fusion.x_ref
  5.0 20.5 %shard_map.93 = bf16[2,8,144,128]{3,2,1,0:T(8,128)(2,1)S(1)} custom-call(bf16[2,8,144,128]{3,2,1,0:T(8,128)(2,1)S(1)} %pad_maximum_fusion.x_ref), custom_call_target="tpu_custom_call" | custom-call | tf_op jit(solution)/shard_map/pallas_call | solution.py:275
  25.5 0.3 reshape.33.x_ref
  25.8 55.3 %shard_map.94 = bf16[2,8,144,1024]{3,2,1,0:T(8,128)(2,1)S(1)} custom-call(bf16[2,144,1024]{2,1,0:T(8,128)(2,1)S(1)} %reshape.33.x_ref), custom_call_target="tpu_custom_call" | custom-call | tf_op jit(solution)/shard_map/pallas_call | solution.py:100
  81.1 0.5 fusion.14
  81.6 0.0 copy-done
  81.6 0.0 copy-start.2
  81.6 1.6 multiply_convert_fusion
  83.2 0.0 copy-done.2
  83.2 2.2 %fusion = bf16[1152,512]{1,0:T(8,128)(2,1)S(1)} fusion(bf16[1152,1024]{1,0:T(8,128)(2,1)S(1)} %bitcast.24, bf16[1024,512]{1,0:T(8,128)(2,1)S(1)} %copy-done.2, f32[1152,512]{1,0:T(8,128)S(1)} %get-tuple-element.19), kind=kOutput, calls=%fused_computation.8 | convolution fusion | flops 1213857792 | bytes 6946816 | tf_op jit(solution)/shard_map/dot_general | solution.py:334
  85.4 1.6 convolution_multiply_fusion.1.gu_ref
  87.0 1.5 convolution_multiply_fusion.2.gd_ref
  88.5 1.4 convolution_convert_fusion
  89.9 1.4 convolution_convert_fusion.1
  91.4 69.2 %shard_map.95 = (bf16[2,144,1024]{2,1,0:T(8,128)(2,1)S(1)}, f32[128,512]{1,0:T(8,128)S(1)}, f32[128,512]{1,0:T(8,128)S(1)}) custom-call(bf16[8,144,1024]{2,1,0:T(8,128)(2,1)S(1)} %bitcast.23, bf16[8,144,1024]{2,1,0:T(8,128)(2,1)S(1)} %bitcast.22, f32[1024,512]{1,0:T(8,128)S(1)} %convolution_multiply_fusion.2.gd_ref, ...), custom_call_target="tpu_custom_call" | custom-call | tf_op jit(solution)/shard_map/pallas_call | solution.py:228
  160.6 0.3 reshape_reshape.3.x_ref
  160.8 17.7 %shard_map.96 = bf16[2,8,144,128]{3,2,1,0:T(8,128)(2,1)S(1)} custom-call(bf16[2,8,144,128]{3,2,1,0:T(8,128)(2,1)S(1)} %reshape_reshape.3.x_ref), custom_call_target="tpu_custom_call" | custom-call | tf_op jit(solution)/shard_map/pallas_call | solution.py:275
  178.6 0.2 squeeze.14
  178.8 0.2 copy.12
  179.0 1.6 gather_fusion
  180.6 0.0 copy-start.1
  180.6 0.2 squeeze.15
  180.8 0.2 copy.13
  180.9 1.6 gather_fusion.1
  182.5 0.0 copy-done.1
  182.6 0.9 broadcast_select_fusion
  183.5 0.7 copy.16
  184.2 0.7 copy.17
  (2 shorter events, 0.0 us)
Async XLA Ops:
  0.6 81.0 %copy-start = (bf16[1024,512]{1,0:T(8,128)(2,1)S(1)}, bf16[1024,512]{1,0:T(8,128)(2,1)}, u32[]{:S(2)}) copy-start(bf16[1024,512]{1,0:T(8,128)(2,1)} %param.10) | copy-start | bytes 3145732
  81.6 1.6 copy-start.2
  180.6 2.0 %copy-start.1 = (s32[128]{0:T(128)S(1)}, s32[128]{0:T(128)}, u32[]{:S(2)}) copy-start(s32[128]{0:T(128)} %param.9) | copy-start | bytes 1540
